TPU v7x, 256 devices: a whole 4x4x8 slice. The times are simulated.
256 devices in a mesh: plane: 2 (over core), row: 8 (over z), col: 16 (over y, x).
Axes of the slice: x: 4, y: 4, z: 8, core: 2. Of those that a mesh axis runs over, the one named last changes fastest.
Arguments:
- velocity: float32 [3, 4, 4096, 4096], P(None, 'plane', 'row', 'col'), may hold values from -60 to 60
Outputs:
- dissipation: float32 [4, 4096, 4096], P('plane', 'row', 'col')
- fine_means: float32 [128, 128], P('row', 'col')
- coarse_means: float32 [4, 4], replicated
All inputs are finite; a program needn't handle non-finite values.
Results may differ from a plain program's by a relative error of at most 0.000078.
Values sent between devices are 32-bit elements; how exact they have to be, the bound alone decides.
No kernel may reach another device: no remote copies, remote signals or barrier semaphores. Data moves between devices by JAX's collectives and lax.ppermute only.
A program may use at most 128 MiB of HBM per device.

v0:
```python
import functools
import math

import jax
import jax.numpy as jnp
import numpy as np
from jax import lax
from jax.experimental import pallas as pl
from jax.experimental.pallas import tpu as pltpu
from jax.sharding import Mesh
from jax.sharding import PartitionSpec as P

N = 4096
FINE = 32
COARSE = 1024
M = 256
ROWS = 8
DISTANCES = (4, 3, 5, 2, 6, 1, 7)
COL = ("col_0", "col_1")
PLANE_COL = ("plane", "col_0", "col_1")
HIGH = lax.Precision.HIGHEST
LIMIT = 20 << 20


def turns():
    turn = 2.0 * math.pi / N * (np.arange(16) - 8)[:, None] * np.arange(M)[None, :]
    tall = np.zeros((2, M, 128), np.float32)
    tall[0, :, :16] = np.cos(turn).T
    tall[1, :, :16] = np.sin(turn).T
    wide = np.stack([np.cos(turn), np.sin(turn)], axis=1)[:, :, None, :]
    return wide.astype(np.float32), tall


def base_kernel(out):
    lag = lax.broadcasted_iota(jnp.int32, (M, M), 0) - lax.broadcasted_iota(jnp.int32, (M, M), 1)
    size = jnp.abs(lag)
    angle = jnp.minimum(size, M - size).astype(jnp.float32) * (math.pi / M)
    scale = jnp.where((lag > 0) == (lax.rem(size, 2) == 0), math.pi / (16 * M), -math.pi / (16 * M))
    out[...] = jnp.where(lag == 0, 0.0, scale / jnp.where(lag == 0, 1.0, jnp.sin(angle)))


def matrices(base, wide, tall, k):
    lane = lax.broadcasted_iota(jnp.int32, (M, 128), 1)
    ca = jnp.sum(jnp.where(lane == k, tall[0], 0.0), axis=1, keepdims=True)
    sa = jnp.sum(jnp.where(lane == k, tall[1], 0.0), axis=1, keepdims=True)
    cb, sb = wide[k, 0], wide[k, 1]
    common = base[...]
    same = lax.broadcasted_iota(jnp.int32, (M, M), 0) == lax.broadcasted_iota(jnp.int32, (M, M), 1)
    middle = (k - 8).astype(jnp.float32) * (2.0 * math.pi / (16 * N))
    imag = common * (sa * cb - ca * sb) + jnp.where(same, middle, 0.0)
    return common * (ca * cb + sa * sb), jnp.where(k == 0, common, imag)


def vmem_call(kernel, outs, scratch=(), smem=0):
    def call(*args):
        specs = [pl.BlockSpec(memory_space=pltpu.SMEM)] * smem
        specs += [pl.BlockSpec(memory_space=pltpu.VMEM)] * (len(args) - smem)
        many = isinstance(outs, (list, tuple))
        out_specs = jax.tree.map(lambda _: pl.BlockSpec(memory_space=pltpu.VMEM), list(outs) if many else outs)
        return pl.pallas_call(
            kernel,
            out_shape=list(outs) if many else outs,
            in_specs=specs,
            out_specs=out_specs,
            scratch_shapes=list(scratch),
            compiler_params=pltpu.CompilerParams(vmem_limit_bytes=LIMIT),
        )(*args)

    return call


def near(values):
    return pltpu.with_memory_space_constraint(values, pltpu.VMEM)


def f32(*shape):
    return jax.ShapeDtypeStruct(shape, jnp.float32)


def real_dft(values):
    n = len(values)
    if n == 2:
        return [(values[0] + values[1], None), (values[0] - values[1], None)]
    even, odd = real_dft(values[0::2]), real_dft(values[1::2])
    half = n // 2
    out = [None] * (half + 1)
    out[0] = (even[0][0] + odd[0][0], None)
    out[half] = (even[0][0] - odd[0][0], None)
    for k in range(1, n // 4):
        angle = 2.0 * math.pi * k / n
        c, s = math.cos(angle), math.sin(angle)
        (er, ei), (orr, oi) = even[k], odd[k]
        if 2 * k * 4 == n:
            tr, ti = (orr + oi) * c, (oi - orr) * c
        else:
            tr, ti = orr * c + oi * s, oi * c - orr * s
        out[k] = (er + tr, ei + ti)
        out[half - k] = (er - tr, ti - ei)
    q = n // 4
    out[q] = (even[q][0], -odd[q][0])
    return out


def real_idft(spec):
    half = len(spec) - 1
    n = 2 * half
    if n == 2:
        return [spec[0][0] + spec[1][0], spec[0][0] - spec[1][0]]
    q = n // 4
    even, odd = [None] * (q + 1), [None] * (q + 1)
    even[0] = (spec[0][0] + spec[half][0], None)
    odd[0] = (spec[0][0] - spec[half][0], None)
    even[q] = (2.0 * spec[q][0], None)
    odd[q] = (-2.0 * spec[q][1], None)
    for k in range(1, q):
        angle = 2.0 * math.pi * k / n
        c, s = math.cos(angle), math.sin(angle)
        (ar, ai), (br, bi) = spec[k], spec[half - k]
        even[k] = (ar + br, ai - bi)
        dr, di = ar - br, ai + bi
        if 8 * k == n:
            odd[k] = ((dr - di) * c, (dr + di) * c)
        else:
            odd[k] = (dr * c - di * s, dr * s + di * c)
    out = [None] * n
    out[0::2] = real_idft(even)
    out[1::2] = real_idft(odd)
    return out


def lane_ids(rows):
    return lax.broadcasted_iota(jnp.int32, (rows, 128), 1)


def swap_lanes(four):
    group = lax.broadcasted_iota(jnp.int32, four[0].shape, 1) // 32
    low, even = group < 2, lax.rem(group, 2) == 0
    a, b, c, d = four
    a, c = jnp.where(low, a, pltpu.roll(c, 64, 1)), jnp.where(low, pltpu.roll(a, 64, 1), c)
    b, d = jnp.where(low, b, pltpu.roll(d, 64, 1)), jnp.where(low, pltpu.roll(b, 64, 1), d)
    a, b = jnp.where(even, a, pltpu.roll(b, 32, 1)), jnp.where(even, pltpu.roll(a, 96, 1), b)
    c, d = jnp.where(even, c, pltpu.roll(d, 32, 1)), jnp.where(even, pltpu.roll(c, 96, 1), d)
    return a, b, c, d


def pack_rows_kernel(row, *refs, count, step=32):
    vels, outs, held = refs[:count], refs[count : count + 8], refs[count + 8]

    def body(i, carry):
        rows = pl.ds(pl.multiple_of(i * step, step), step)
        later = pl.ds(pl.multiple_of(i * step + 256, step), step)
        for n, vel in enumerate(vels):
            for t in range(2):
                lanes = pl.ds(t * 128, 128)
                four = swap_lanes([vel[0, p, r, lanes] for r in (rows, later) for p in range(2)])
                for off in range(4):
                    held[4 * t + off, n, rows, :] = four[off]
        return carry

    lax.fori_loop(0, 256 // step, body, 0)
    for dist in range(ROWS):
        outs[dist][...] = held[lax.rem(row[0] + dist, ROWS)]


def pack_rows(row, velocity, comps):
    count = len(comps)
    whole = pl.BlockSpec((count, 256, 128), lambda i: (0, 0, 0))

    def one(c):
        return pl.BlockSpec((1, 2, 512, 256), lambda i: (c, 0, 0, 0))

    return pl.pallas_call(
        functools.partial(pack_rows_kernel, count=count),
        out_shape=[f32(count, 256, 128)] * ROWS,
        grid=(1,),
        in_specs=[pl.BlockSpec(memory_space=pltpu.SMEM)] + [one(c) for c in comps],
        out_specs=[whole] * ROWS,
        scratch_shapes=[pltpu.VMEM((ROWS, count, 256, 128), jnp.float32)],
        name="pack_rows",
        compiler_params=pltpu.CompilerParams(vmem_limit_bytes=LIMIT),
    )(row, *([velocity] * count))


def hold_blocks(row, blocks, held):
    for dist in range(ROWS):
        held[lax.rem(row[0] + dist, ROWS)] = blocks[dist][0]


def home_tiles(held, rows, t):
    four = swap_lanes([held[4 * t + off, rows, :] for off in range(4)])
    return {(half, p): four[2 * half + p] for half in range(2) for p in range(2)}


def send_blocks(blocks):
    got = [blocks[0]] + [None] * (ROWS - 1)
    for dist in DISTANCES:
        perm = [(i, (i + dist) % ROWS) for i in range(ROWS)]
        got[(ROWS - dist) % ROWS] = lax.ppermute(blocks[dist], "row", perm)
    return got


def spectral_x(tables, spec, res):
    def body(k, carry):
        lone = k == 0
        first, second = matrices(*tables, k)
        a = jnp.dot(first, spec[k], precision=HIGH)
        b = jnp.dot(second, spec[k], precision=HIGH)
        res[k, :, :128] = a[:, :128] - jnp.where(lone, 0.0, b[:, 128:])
        res[k, :, 128:] = jnp.where(lone, b[:, 128:], a[:, 128:] + b[:, :128])
        return carry

    lax.fori_loop(0, 8, body, 0, unroll=2)


STEP = 16


def store_spec(spec, freq, rows):
    for k in range(8):
        re, im = freq[k]
        spec[k, rows, :128] = re
        spec[k, rows, 128:] = freq[8][0] if k == 0 else im


def load_spec(res, rows):
    freq = [(res[k, rows, :128], res[k, rows, 128:]) for k in range(8)]
    return [(freq[0][0], None)] + freq[1:] + [(freq[0][1], None)]


def grad_v_kernel(*refs):
    tables, refs = refs[:3], refs[3:]
    blocks, outs, spec, res = refs[:8], refs[8:16], refs[16], refs[17]
    low = lane_ids(STEP) < 64

    def forward(i, carry):
        rows = pl.ds(pl.multiple_of(i * STEP, STEP), STEP)
        values = []
        for j in range(8):
            src = blocks[j][0, rows, :]
            values += [src, pltpu.roll(src, 64, 1)]
        store_spec(spec, real_dft(values), rows)
        return carry

    lax.fori_loop(0, 256 // STEP, forward, 0)
    spectral_x(tables, spec, res)

    def backward(i, carry):
        rows = pl.ds(pl.multiple_of(i * STEP, STEP), STEP)
        values = real_idft(load_spec(res, rows))
        for j in range(8):
            outs[j][0, rows, :] = jnp.where(low, values[2 * j], pltpu.roll(values[2 * j + 1], 64, 1))
        return carry

    lax.fori_loop(0, 256 // STEP, backward, 0)


X_SCRATCH = (pltpu.VMEM((8, 256, 256), jnp.float32), pltpu.VMEM((8, 256, 256), jnp.float32))


def grad_v(tables, blocks):
    return vmem_call(grad_v_kernel, [f32(1, 256, 128)] * 8, X_SCRATCH)(*tables, *blocks)


def stack_first_kernel(*refs):
    for j in range(8):
        refs[8][j] = refs[j][0]


def stack_first(blocks):
    one = pl.BlockSpec((1, 256, 128), lambda i: (0, 0, 0))
    return pl.pallas_call(
        stack_first_kernel,
        out_shape=f32(8, 256, 128),
        grid=(1,),
        in_specs=[one] * 8,
        out_specs=pl.BlockSpec((8, 256, 128), lambda i: (0, 0, 0)),
        name="stack_first",
        compiler_params=pltpu.CompilerParams(vmem_limit_bytes=LIMIT),
    )(*blocks)


def grad_uw_kernel(row, *refs):
    tables, refs = refs[:3], refs[3:]
    blocks, other, out, sums, spec, res = refs[:8], *refs[8:]
    lane = lane_ids(STEP)
    low = lane < 64
    first = lax.rem(lane // 32, 2) == 0

    def forward(i, carry):
        rows = pl.ds(pl.multiple_of(i * STEP, STEP), STEP)
        values = []
        for j in range(8):
            u, w = blocks[j][0, rows, :], blocks[j][1, rows, :]
            values += [jnp.where(low, u, pltpu.roll(w, 64, 1)), jnp.where(low, pltpu.roll(u, 64, 1), w)]
        store_spec(spec, real_dft(values), rows)
        return carry

    lax.fori_loop(0, 256 // STEP, forward, 0)
    spectral_x(tables, spec, res)

    def backward(i, carry):
        rows = pl.ds(pl.multiple_of(i * STEP, STEP), STEP)
        values = real_idft(load_spec(res, rows))
        totals = []
        for j in range(8):
            a, b = values[2 * j], values[2 * j + 1]
            u_x = jnp.where(low, a, pltpu.roll(b, 64, 1))
            w_x = jnp.where(low, pltpu.roll(a, 64, 1), b)
            diff = blocks[j][0, rows, :] - other[j, rows, :]
            u_z = 0.5 * jnp.where(first, pltpu.roll(diff, 96, 1), -pltpu.roll(diff, 32, 1))
            cross = u_z + w_x
            part = u_x * u_x + 0.5 * (cross * cross)
            out[lax.rem(row[0] + j, ROWS), rows, :] = part
            totals.append(carry[j] + part)
        return tuple(totals)

    zero = jnp.zeros((STEP, 128), jnp.float32)
    totals = lax.fori_loop(0, 256 // STEP, backward, (zero,) * 8)
    for j in range(8):
        sums[j : j + 1, :] = jnp.sum(totals[j], axis=0, keepdims=True)


def grad_uw(row, tables, other, blocks):
    outs = [f32(8, 256, 128), f32(8, 128)]
    return vmem_call(grad_uw_kernel, outs, X_SCRATCH, smem=1)(row, *tables, *blocks, other)


def grad_y_kernel(base, wide, tall, data, out, spec, res):
    tables = (base, wide, tall)

    def forward(i, carry):
        c = i // 16
        k = lax.rem(i // 8, 2)
        p = lax.rem(i // 4, 2)
        half = pl.ds(pl.multiple_of(lax.rem(i // 2, 2) * 8, 8), 8)
        lanes = pl.ds(pl.multiple_of(lax.rem(i, 2) * 128, 128), 128)
        rows = pl.multiple_of((i // 2) * 8, 8)
        freq = real_dft([data[k, b, c, p, half, lanes] for b in range(16)])
        for f in range(8):
            spec[f, pl.ds(rows, 8), lanes] = freq[f][0]
            spec[f, pl.ds(rows + 192, 8), lanes] = freq[8][0] if f == 0 else freq[f][1]
        return carry

    lax.fori_loop(0, 48, forward, 0)

    def middle(f, carry):
        lone = f == 0
        first, second = matrices(*tables, f)
        a = jnp.dot(spec[f], first, precision=HIGH)
        b = jnp.dot(spec[f], second, precision=HIGH)
        res[f, :192] = -a[:192] - jnp.where(lone, 0.0, b[192:])
        res[f, 192:] = jnp.where(lone, -b[192:], b[:192] - a[192:])
        return carry

    lax.fori_loop(0, 8, middle, 0, unroll=2)

    def backward(i, carry):
        k = i // 4
        half = pl.ds(pl.multiple_of(lax.rem(i // 2, 2) * 8, 8), 8)
        lanes = pl.ds(pl.multiple_of(lax.rem(i, 2) * 128, 128), 128)
        for p in range(2):

            def slope(c):
                start = pl.multiple_of(c * 64 + k * 32 + p * 16 + lax.rem(i // 2, 2) * 8, 8)
                freq = [(res[f, pl.ds(start, 8), lanes], res[f, pl.ds(start + 192, 8), lanes]) for f in range(8)]
                return real_idft([(freq[0][0], None)] + freq[1:] + [(freq[0][1], None)])

            def slope_z(c, b):
                gap = data[k, b, c, 1 - p, half, lanes] - data[1 - k, b, c, 1 - p, half, lanes]
                return gap * (0.5 if p == 0 else -0.5)

            for b, value in enumerate(slope(0)):
                out[k, b, 1, p, half, lanes] = value
            for b, value in enumerate(slope(1)):
                w_z = slope_z(2, b)
                out[k, b, 0, p, half, lanes] = value * value + w_z * w_z
            for b, value in enumerate(slope(2)):
                cross = slope_z(1, b) + value
                out[k, b, 0, p, half, lanes] += 0.5 * (cross * cross)
        return carry

    lax.fori_loop(0, 8, backward, 0)


def grad_y(tables, data):
    scratch = (pltpu.VMEM((8, 384, 256), jnp.float32), pltpu.VMEM((8, 384, 256), jnp.float32))
    return vmem_call(grad_y_kernel, f32(2, 16, 2, 2, 16, 256), scratch)(*tables, near(data))


def pack_cols_kernel(vel, out):
    def body(g, carry):
        start = pl.multiple_of(g * 16, 16)
        for c in range(3):
            for p in range(2):
                out[g, c, p] = vel[c, p, pl.ds(start, 16), :]
        return carry

    lax.fori_loop(0, 32, body, 0)


def partial_kernel(place, y_terms, x_sums, *refs):
    blocks, out, boxes, held = refs[:8], refs[8], refs[9], refs[10]
    hold_blocks(place, blocks, held)

    def body(i, carry):
        rows = pl.ds(pl.multiple_of(i * 16, 16), 16)
        for t in range(2):
            lanes = pl.ds(t * 128, 128)
            for (half, p), v_x in home_tiles(held, rows, t).items():
                g = i + 16 * half
                cross = y_terms[g, 1, p, :, lanes] + v_x
                value = y_terms[g, 0, p, :, lanes] + 0.5 * (cross * cross)
                out[p, pl.ds(pl.multiple_of(g * 16, 16), 16), lanes] = value
                carry = carry + value
        return carry

    total = lax.fori_loop(0, 16, body, jnp.zeros((16, 128), jnp.float32))
    down = lax.broadcasted_iota(jnp.int32, (8, 128), 0)
    mine = lax.broadcasted_iota(jnp.int32, (8, 128), 1) == place[1] // 4
    zero = jnp.zeros((8, 128), jnp.float32)
    found = jnp.where(down == place[0] // 2, jnp.sum(total), zero)
    for j in range(ROWS):
        box = lax.rem(place[0] + j, ROWS) // 2
        found = found + jnp.where(down == box, jnp.sum(x_sums[j : j + 1, :]), zero)
    boxes[...] = jnp.where(mine, found * (1.0 / (4 * COARSE * COARSE)), zero)


def final_kernel(part, held, out, boxes, lines):

    def body(a, carry):
        rows = pl.ds(pl.multiple_of(a * 32, 32), 32)
        for t in range(2):
            lanes = pl.ds(t * 128, 128)
            tiles = home_tiles(held, rows, t)
            for half in range(2):
                there = pl.ds(pl.multiple_of(a * 32 + 256 * half, 32), 32)
                first = part[0, there, lanes] + tiles[half, 0]
                second = part[1, there, lanes] + tiles[half, 1]
                out[0, there, lanes] = first
                out[1, there, lanes] = second
                total = (first + second).reshape(4, 8, 128).sum(axis=0)
                lines[a + 8 * half, :, lanes] = total
        return carry

    lax.fori_loop(0, 8, body, 0)
    cell = lax.broadcasted_iota(jnp.int32, (256, 128), 0) // FINE
    select = jnp.where(cell == lax.broadcasted_iota(jnp.int32, (256, 128), 1), 1.0 / (4 * FINE * FINE), 0.0)
    boxes[...] = jnp.dot(jnp.sum(lines[...], axis=1), select, precision=HIGH)


def whole_step(velocity):
    row = lax.axis_index("row")
    col = lax.axis_index(COL)
    row_arg = row.astype(jnp.int32).reshape(1)
    for_cols = vmem_call(pack_cols_kernel, f32(32, 3, 2, 16, 256))(velocity)
    lines = lax.all_to_all(for_cols, PLANE_COL, split_axis=0, concat_axis=0, tiled=True)
    v_blocks = pack_rows(row_arg, velocity, (1,))
    v_blocks = send_blocks(v_blocks)
    uw_blocks = pack_rows(row_arg, velocity, (0, 2))
    uw_blocks = send_blocks(uw_blocks)
    tables = (vmem_call(base_kernel, f32(M, M))(), *(jnp.asarray(a) for a in turns()))
    v_x = grad_v(tables, v_blocks)
    v_x = send_blocks(v_x)
    y_terms = grad_y(tables, lines.reshape(2, 16, 3, 2, 16, 256))
    y_terms = lax.all_to_all(
        y_terms.reshape(32, 2, 2, 16, 256), PLANE_COL, split_axis=0, concat_axis=0, tiled=True
    )
    other = stack_first(uw_blocks)
    other = lax.ppermute(other, "plane", [(0, 1), (1, 0)])
    x_terms, x_sums = grad_uw(row_arg, tables, other, uw_blocks)
    x_terms = lax.all_to_all(x_terms, "row", split_axis=0, concat_axis=0, tiled=True)
    held = pltpu.VMEM((ROWS, 256, 128), jnp.float32)
    place = jnp.stack([row, col]).astype(jnp.int32)
    part, coarse = vmem_call(partial_kernel, [f32(2, 512, 256), f32(8, 128)], (held,), smem=1)(
        place, near(y_terms), x_sums, *v_x
    )
    coarse = sum_of_four(coarse, "col_1", lambda i, n: (i + (2, 1, 3)[n]) % 4)
    coarse = sum_of_four(coarse, "col_0", lambda i, n: (i + (2, 1, 3)[n]) % 4)
    coarse = sum_of_four(coarse, ("plane", "row"), lambda i, n: i ^ (8, 1, 9)[n])
    coarse = sum_of_four(coarse, "row", lambda i, n: (i + (4, 2, 6)[n]) % 8)
    coarse = coarse[:4, :4]
    dissip, fine = vmem_call(
        final_kernel,
        [f32(2, 512, 256), f32(16, 128)],
        (pltpu.VMEM((16, 8, 256), jnp.float32),),
    )(part, near(x_terms))
    fine = (fine + lax.ppermute(fine, "plane", [(0, 1), (1, 0)]))[:, :8]
    return dissip, fine, coarse


def sum_of_four(values, axis, partner):
    size = lax.axis_size(axis)
    got = [lax.ppermute(values, axis, [(i, partner(i, n)) for i in range(size)]) for n in range(3)]
    return (values + got[0]) + (got[1] + got[2])


def solution(mesh):
    split = Mesh(
        mesh.devices.reshape(mesh.shape["plane"], mesh.shape["row"], 4, 4),
        ("plane", "row", "col_0", "col_1"),
    )
    in_specs = (P(None, "plane", "row", COL),)
    out_specs = (P("plane", "row", COL), P("row", COL), P())
    return jax.shard_map(whole_step, mesh=split, in_specs=in_specs, out_specs=out_specs, check_vma=False)
```

profile of v0, /device:TPU:2, one launch (start us, length us, event | category | flops | bytes accessed | tf_op | source)
XLA Modules:
  0.0 276.9 jit_solution(4111546100550215765)
XLA Ops:
  4.4 7.7 %all-to-all-start = ((f32[32,3,2,16,256]{4,3,2,1,0:T(8,128)}), f32[32,3,2,16,256]{4,3,2,1,0:T(8,128)S(1)}, u32[]{:S(2)}, u32[]{:S(2)}) async-start(f32[32,3,2,16,256]{4,3,2,1,0:T(8,128)} %copy-done.2), calls=%async_computation | async-start | bytes 6291456 | tf_op jit(solution)/shard_map/all_to_all | solution.py:456
  13.2 37.9 %all-to-all-done = f32[32,3,2,16,256]{4,3,2,1,0:T(8,128)S(1)} async-done(((f32[32,3,2,16,256]{4,3,2,1,0:T(8,128)}), f32[32,3,2,16,256]{4,3,2,1,0:T(8,128)S(1)}, u32[]{:S(2)}, u32[]{:S(2)}) %all-to-all-start) | async-done | bytes 3145760 | tf_op jit(solution)/shard_map/all_to_all | solution.py:456
  52.1 10.1 %shard_map.60 = f32[2,16,2,2,16,256]{5,4,3,2,1,0:T(8,128)S(1)} custom-call(f32[256,256]{1,0:T(8,128)S(1)} %shard_map.58.base.refs_0_, f32[16,2,1,256]{3,2,1,0:T(1,128)S(1)} %copy-done.8, f32[2,256,128]{2,1,0:T(8,128)S(1)} %copy-done.4, f32[2,16,3,2,16,256]{5,4,3,2,1,0:T(8,128)S(1)} %bitcast.4), custom_call_target="tpu_custom_call" | custom-call | tf_op jit(solution)/shard_map/pallas_call | solution.py:60
  63.6 7.0 %all-to-all-start.1 = ((f32[32,2,2,16,256]{4,3,2,1,0:T(8,128)}), f32[32,2,2,16,256]{4,3,2,1,0:T(8,128)}, u32[]{:S(2)}, u32[]{:S(2)}) async-start(f32[32,2,2,16,256]{4,3,2,1,0:T(8,128)} %bitcast.5), calls=%async_computation.1 | async-start | bytes 4194304 | tf_op jit(solution)/shard_map/all_to_all | solution.py:465
  73.1 5.9 %collective-permute-start = (f32[2,256,128]{2,1,0:T(8,128)S(1)}, f32[2,256,128]{2,1,0:T(8,128)S(1)}, u32[]{:S(2)}, u32[]{:S(2)}) collective-permute-start(f32[2,256,128]{2,1,0:T(8,128)S(1)} %get-tuple-element.34), channel_id=1, source_target_pairs={{0,112},{16,0},{32,16},{48,32},{64,48},{80,64},{96,80},{112,96},{1... | collective-permute-start | bytes 786440 | tf_op jit(solution)/shard_map/ppermute | solution.py:198
  80.9 5.0 %collective-permute-start.3 = (f32[2,256,128]{2,1,0:T(8,128)S(1)}, f32[2,256,128]{2,1,0:T(8,128)S(1)}, u32[]{:S(2)}, u32[]{:S(2)}) collective-permute-start(f32[2,256,128]{2,1,0:T(8,128)S(1)} %get-tuple-element.37), channel_id=1, source_target_pairs={{0,64},{16,80},{32,96},{48,112},{64,0},{80,16},{96,32},{112,48},{1... | collective-permute-start | bytes 786440 | tf_op jit(solution)/shard_map/ppermute | solution.py:198
  85.9 6.5 %collective-permute-done.refs_1_.refs_4_ = f32[2,256,128]{2,1,0:T(8,128)S(1)} collective-permute-done((f32[2,256,128]{2,1,0:T(8,128)S(1)}, f32[2,256,128]{2,1,0:T(8,128)S(1)}, u32[]{:S(2)}, u32[]{:S(2)}) %collective-permute-start) | collective-permute-done | bytes 262176 | tf_op jit(solution)/shard_map/ppermute | solution.py:198
  92.4 12.7 %collective-permute-done.1.refs_2_.refs_5_ = f32[2,256,128]{2,1,0:T(8,128)S(1)} collective-permute-done((f32[2,256,128]{2,1,0:T(8,128)S(1)}, f32[2,256,128]{2,1,0:T(8,128)S(1)}, u32[]{:S(2)}, u32[]{:S(2)}) %collective-permute-start.1) | collective-permute-done | bytes 262176 | tf_op jit(solution)/shard_map/ppermute | solution.py:198
  105.1 19.2 %collective-permute-done.2.refs_3_.refs_6_ = f32[2,256,128]{2,1,0:T(8,128)S(1)} collective-permute-done((f32[2,256,128]{2,1,0:T(8,128)S(1)}, f32[2,256,128]{2,1,0:T(8,128)S(1)}, u32[]{:S(2)}, u32[]{:S(2)}) %collective-permute-start.2) | collective-permute-done | bytes 262176 | tf_op jit(solution)/shard_map/ppermute | solution.py:198
  124.3 3.9 %collective-permute-done.5.refs_6_.refs_9_ = f32[2,256,128]{2,1,0:T(8,128)S(1)} collective-permute-done((f32[2,256,128]{2,1,0:T(8,128)S(1)}, f32[2,256,128]{2,1,0:T(8,128)S(1)}, u32[]{:S(2)}, u32[]{:S(2)}) %collective-permute-start.5) | collective-permute-done | bytes 262176 | tf_op jit(solution)/shard_map/ppermute | solution.py:198
  128.2 3.7 %collective-permute-done.6.refs_7_.refs_10_ = f32[2,256,128]{2,1,0:T(8,128)S(1)} collective-permute-done((f32[2,256,128]{2,1,0:T(8,128)S(1)}, f32[2,256,128]{2,1,0:T(8,128)S(1)}, u32[]{:S(2)}, u32[]{:S(2)}) %collective-permute-start.6) | collective-permute-done | bytes 262176 | tf_op jit(solution)/shard_map/ppermute | solution.py:198
  132.1 2.6 collective-permute-done.7.refs_11_
  134.7 9.3 %shard_map.61 = (f32[8,256,128]{2,1,0:T(8,128)S(1)}, f32[8,128]{1,0:T(8,128)S(1)}) custom-call(s32[1]{0:T(128)} %bitcast.row, f32[256,256]{1,0:T(8,128)S(1)} %shard_map.58.base.refs_0_, f32[16,2,1,256]{3,2,1,0:T(1,128)S(1)} %copy-done.8, f32[2,256,128]{2,1,0:T(8,128)S(1)} %copy-done.5, f32[2,256,128]{2,1,0:T(8,128)S(1)} %get-tuple-element.33.refs_0_.refs_3_, ...), custom_call_target="tpu_custom_call" | custom-call | tf_op jit(solution)/shard_map/pallas_call | solution.py:60
  145.0 4.2 %all-to-all-start.2 = ((f32[8,256,128]{2,1,0:T(8,128)}), f32[8,256,128]{2,1,0:T(8,128)}, u32[]{:S(2)}, u32[]{:S(2)}) async-start(f32[8,256,128]{2,1,0:T(8,128)} %copy-done.7), calls=%async_computation.2 | async-start | bytes 2097152 | tf_op jit(solution)/shard_map/all_to_all | solution.py:471
  150.9 3.4 %collective-permute-start.8 = (f32[1,256,128]{2,1,0:T(8,128)S(1)}, f32[1,256,128]{2,1,0:T(8,128)S(1)}, u32[]{:S(2)}, u32[]{:S(2)}) collective-permute-start(f32[1,256,128]{2,1,0:T(8,128)S(1)} %get-tuple-element.43), channel_id=1, source_target_pairs={{0,112},{16,0},{32,16},{48,32},{64,48},{80,64},{96,80},{112,96},{1... | collective-permute-start | bytes 393224 | tf_op jit(solution)/shard_map/ppermute | solution.py:198
  158.0 3.6 %collective-permute-start.11 = (f32[1,256,128]{2,1,0:T(8,128)S(1)}, f32[1,256,128]{2,1,0:T(8,128)S(1)}, u32[]{:S(2)}, u32[]{:S(2)}) collective-permute-start(f32[1,256,128]{2,1,0:T(8,128)S(1)} %get-tuple-element.46), channel_id=1, source_target_pairs={{0,64},{16,80},{32,96},{48,112},{64,0},{80,16},{96,32},{112,48},{1... | collective-permute-start | bytes 393224 | tf_op jit(solution)/shard_map/ppermute | solution.py:198
  161.9 17.0 %collective-permute-done.8.refs_4_ = f32[1,256,128]{2,1,0:T(8,128)S(1)} collective-permute-done((f32[1,256,128]{2,1,0:T(8,128)S(1)}, f32[1,256,128]{2,1,0:T(8,128)S(1)}, u32[]{:S(2)}, u32[]{:S(2)}) %collective-permute-start.8) | collective-permute-done | bytes 131104 | tf_op jit(solution)/shard_map/ppermute | solution.py:198
  180.5 6.9 %collective-permute-done.9.refs_5_ = f32[1,256,128]{2,1,0:T(8,128)S(1)} collective-permute-done((f32[1,256,128]{2,1,0:T(8,128)S(1)}, f32[1,256,128]{2,1,0:T(8,128)S(1)}, u32[]{:S(2)}, u32[]{:S(2)}) %collective-permute-start.9) | collective-permute-done | bytes 131104 | tf_op jit(solution)/shard_map/ppermute | solution.py:198
  187.4 5.8 %collective-permute-done.10.refs_6_ = f32[1,256,128]{2,1,0:T(8,128)S(1)} collective-permute-done((f32[1,256,128]{2,1,0:T(8,128)S(1)}, f32[1,256,128]{2,1,0:T(8,128)S(1)}, u32[]{:S(2)}, u32[]{:S(2)}) %collective-permute-start.10) | collective-permute-done | bytes 131104 | tf_op jit(solution)/shard_map/ppermute | solution.py:198
  193.3 3.5 %collective-permute-done.13.refs_9_ = f32[1,256,128]{2,1,0:T(8,128)S(1)} collective-permute-done((f32[1,256,128]{2,1,0:T(8,128)S(1)}, f32[1,256,128]{2,1,0:T(8,128)S(1)}, u32[]{:S(2)}, u32[]{:S(2)}) %collective-permute-start.13) | collective-permute-done | bytes 131104 | tf_op jit(solution)/shard_map/ppermute | solution.py:198
  198.2 8.1 %shard_map.62 = (f32[1,256,128]{2,1,0:T(8,128)S(1)}, f32[1,256,128]{2,1,0:T(8,128)S(1)}, f32[1,256,128]{2,1,0:T(8,128)S(1)}, f32[1,256,128]{2,1,0:T(8,128)S(1)},...) custom-call(f32[256,256]{1,0:T(8,128)S(1)} %shard_map.58.base.refs_0, ...), custom_call_target="tpu_custom_call" | custom-call | tf_op jit(solution)/shard_map/pallas_call | solution.py:60
  211.5 3.8 %collective-permute-start.18 = (f32[1,256,128]{2,1,0:T(8,128)S(1)}, f32[1,256,128]{2,1,0:T(8,128)S(1)}, u32[]{:S(2)}, u32[]{:S(2)}) collective-permute-start(f32[1,256,128]{2,1,0:T(8,128)S(1)} %get-tuple-element.54), channel_id=1, source_target_pairs={{0,64},{16,80},{32,96},{48,112},{64,0},{80,16},{96,32},{112,48},{1... | collective-permute-start | bytes 393224 | tf_op jit(solution)/shard_map/ppermute | solution.py:198
  215.3 3.3 %collective-permute-start.19 = (f32[1,256,128]{2,1,0:T(8,128)S(1)}, f32[1,256,128]{2,1,0:T(8,128)S(1)}, u32[]{:S(2)}, u32[]{:S(2)}) collective-permute-start(f32[1,256,128]{2,1,0:T(8,128)S(1)} %get-tuple-element.55), channel_id=1, source_target_pairs={{0,48},{16,64},{32,80},{48,96},{64,112},{80,0},{96,16},{112,32},{1... | collective-permute-start | bytes 393224 | tf_op jit(solution)/shard_map/ppermute | solution.py:198
  219.4 6.6 %collective-permute-done.16.refs_2_ = f32[1,256,128]{2,1,0:T(8,128)S(1)} collective-permute-done((f32[1,256,128]{2,1,0:T(8,128)S(1)}, f32[1,256,128]{2,1,0:T(8,128)S(1)}, u32[]{:S(2)}, u32[]{:S(2)}) %collective-permute-start.16) | collective-permute-done | bytes 131104 | tf_op jit(solution)/shard_map/ppermute | solution.py:198
  228.4 5.3 %collective-permute-done.19.refs_5_ = f32[1,256,128]{2,1,0:T(8,128)S(1)} collective-permute-done((f32[1,256,128]{2,1,0:T(8,128)S(1)}, f32[1,256,128]{2,1,0:T(8,128)S(1)}, u32[]{:S(2)}, u32[]{:S(2)}) %collective-permute-start.19) | collective-permute-done | bytes 131104 | tf_op jit(solution)/shard_map/ppermute | solution.py:198
  234.8 4.0 %collective-permute-done.21.refs_7_ = f32[1,256,128]{2,1,0:T(8,128)S(1)} collective-permute-done((f32[1,256,128]{2,1,0:T(8,128)S(1)}, f32[1,256,128]{2,1,0:T(8,128)S(1)}, u32[]{:S(2)}, u32[]{:S(2)}) %collective-permute-start.21) | collective-permute-done | bytes 131104 | tf_op jit(solution)/shard_map/ppermute | solution.py:198
  238.8 4.4 %shard_map.63 = (f32[2,512,256]{2,1,0:T(8,128)S(1)}, f32[8,128]{1,0:T(8,128)S(1)}) custom-call(s32[2]{0:T(128)S(1)} %pad_add_fusion.place, f32[32,2,2,16,256]{4,3,2,1,0:T(8,128)} %all-to-all-done.1.y_terms, f32[8,128]{1,0:T(8,128)S(1)} %get-tuple-element.41.x_sums, f32[1,256,128]{2,1,0:T(8,128)S(1)} %get-tuple-element.50.refs_0_, ...), custom_call_target="tpu_custom_call" | custom-call | tf_op jit(solution)/shard_map/pallas_call | solution.py:60
  255.6 3.2 %collective-permute-done.26 = f32[8,128]{1,0:T(8,128)S(1)} collective-permute-done((f32[8,128]{1,0:T(8,128)S(1)}, f32[8,128]{1,0:T(8,128)S(1)}, u32[]{:S(2)}, u32[]{:S(2)}) %collective-permute-start.26) | collective-permute-done | bytes 4128 | tf_op jit(solution)/shard_map/ppermute | solution.py:493
  261.0 3.6 %shard_map.64 = (f32[2,512,256]{2,1,0:T(8,128)}, f32[16,128]{1,0:T(8,128)S(1)}) custom-call(f32[2,512,256]{2,1,0:T(8,128)S(1)} %get-tuple-element.58.part, f32[8,256,128]{2,1,0:T(8,128)} %all-to-all-done.2.held), custom_call_target="tpu_custom_call" | custom-call | tf_op jit(solution)/shard_map/pallas_call | solution.py:60
  265.6 3.2 %collective-permute-start.34 = (f32[8,128]{1,0:T(8,128)S(1)}, f32[8,128]{1,0:T(8,128)S(1)}, u32[]{:S(2)}, u32[]{:S(2)}) collective-permute-start(f32[8,128]{1,0:T(8,128)S(1)} %add_add_fusion.1), channel_id=1, source_target_pairs={{0,96},{16,112},{32,0},{48,16},{64,32},{80,48},{96,64},{112,80},{1... | collective-permute-start | bytes 12296 | tf_op jit(solution)/shard_map/ppermute | solution.py:493
  268.8 3.7 %collective-permute-start.32 = (f32[8,128]{1,0:T(8,128)S(1)}, f32[8,128]{1,0:T(8,128)S(1)}, u32[]{:S(2)}, u32[]{:S(2)}) collective-permute-start(f32[8,128]{1,0:T(8,128)S(1)} %add_add_fusion.1), channel_id=1, source_target_pairs={{0,64},{16,80},{32,96},{48,112},{64,0},{80,16},{96,32},{112,48},{1... | collective-permute-start | bytes 12296 | tf_op jit(solution)/shard_map/ppermute | solution.py:493
  273.2 3.1 %collective-permute-done.32 = f32[8,128]{1,0:T(8,128)S(1)} collective-permute-done((f32[8,128]{1,0:T(8,128)S(1)}, f32[8,128]{1,0:T(8,128)S(1)}, u32[]{:S(2)}, u32[]{:S(2)}) %collective-permute-start.32) | collective-permute-done | bytes 4128 | tf_op jit(solution)/shard_map/ppermute | solution.py:493
  (80 shorter events, 47.6 us)
Async XLA Ops:
  4.4 46.7 %all-to-all-start = ((f32[32,3,2,16,256]{4,3,2,1,0:T(8,128)}), f32[32,3,2,16,256]{4,3,2,1,0:T(8,128)S(1)}, u32[]{:S(2)}, u32[]{:S(2)}) async-start(f32[32,3,2,16,256]{4,3,2,1,0:T(8,128)} %copy-done.2), calls=%async_computation | async-start | bytes 6291456 | tf_op jit(solution)/shard_map/all_to_all | solution.py:456
  63.6 81.4 %all-to-all-start.1 = ((f32[32,2,2,16,256]{4,3,2,1,0:T(8,128)}), f32[32,2,2,16,256]{4,3,2,1,0:T(8,128)}, u32[]{:S(2)}, u32[]{:S(2)}) async-start(f32[32,2,2,16,256]{4,3,2,1,0:T(8,128)} %bitcast.5), calls=%async_computation.1 | async-start | bytes 4194304 | tf_op jit(solution)/shard_map/all_to_all | solution.py:465
  73.1 19.3 %collective-permute-start = (f32[2,256,128]{2,1,0:T(8,128)S(1)}, f32[2,256,128]{2,1,0:T(8,128)S(1)}, u32[]{:S(2)}, u32[]{:S(2)}) collective-permute-start(f32[2,256,128]{2,1,0:T(8,128)S(1)} %get-tuple-element.34), channel_id=1, source_target_pairs={{0,112},{16,0},{32,16},{48,32},{64,48},{80,64},{96,80},{112,96},{1... | collective-permute-start | bytes 786440 | tf_op jit(solution)/shard_map/ppermute | solution.py:198
  79.0 26.1 %collective-permute-start.1 = (f32[2,256,128]{2,1,0:T(8,128)S(1)}, f32[2,256,128]{2,1,0:T(8,128)S(1)}, u32[]{:S(2)}, u32[]{:S(2)}) collective-permute-start(f32[2,256,128]{2,1,0:T(8,128)S(1)} %get-tuple-element.35), channel_id=1, source_target_pairs={{0,96},{16,112},{32,0},{48,16},{64,32},{80,48},{96,64},{112,80},{1... | collective-permute-start | bytes 786440 | tf_op jit(solution)/shard_map/ppermute | solution.py:198
  80.5 43.8 %collective-permute-start.2 = (f32[2,256,128]{2,1,0:T(8,128)S(1)}, f32[2,256,128]{2,1,0:T(8,128)S(1)}, u32[]{:S(2)}, u32[]{:S(2)}) collective-permute-start(f32[2,256,128]{2,1,0:T(8,128)S(1)} %get-tuple-element.36), channel_id=1, source_target_pairs={{0,80},{16,96},{32,112},{48,0},{64,16},{80,32},{96,48},{112,64},{1... | collective-permute-start | bytes 786440 | tf_op jit(solution)/shard_map/ppermute | solution.py:198
  80.9 43.4 %collective-permute-start.3 = (f32[2,256,128]{2,1,0:T(8,128)S(1)}, f32[2,256,128]{2,1,0:T(8,128)S(1)}, u32[]{:S(2)}, u32[]{:S(2)}) collective-permute-start(f32[2,256,128]{2,1,0:T(8,128)S(1)} %get-tuple-element.37), channel_id=1, source_target_pairs={{0,64},{16,80},{32,96},{48,112},{64,0},{80,16},{96,32},{112,48},{1... | collective-permute-start | bytes 786440 | tf_op jit(solution)/shard_map/ppermute | solution.py:198
  85.9 38.3 %collective-permute-start.4 = (f32[2,256,128]{2,1,0:T(8,128)S(1)}, f32[2,256,128]{2,1,0:T(8,128)S(1)}, u32[]{:S(2)}, u32[]{:S(2)}) collective-permute-start(f32[2,256,128]{2,1,0:T(8,128)S(1)} %get-tuple-element.38), channel_id=1, source_target_pairs={{0,48},{16,64},{32,80},{48,96},{64,112},{80,0},{96,16},{112,32},{1... | collective-permute-start | bytes 786440 | tf_op jit(solution)/shard_map/ppermute | solution.py:198
  92.4 35.8 %collective-permute-start.5 = (f32[2,256,128]{2,1,0:T(8,128)S(1)}, f32[2,256,128]{2,1,0:T(8,128)S(1)}, u32[]{:S(2)}, u32[]{:S(2)}) collective-permute-start(f32[2,256,128]{2,1,0:T(8,128)S(1)} %get-tuple-element.39), channel_id=1, source_target_pairs={{0,32},{16,48},{32,64},{48,80},{64,96},{80,112},{96,0},{112,16},{1... | collective-permute-start | bytes 786440 | tf_op jit(solution)/shard_map/ppermute | solution.py:198
  105.1 26.8 %collective-permute-start.6 = (f32[2,256,128]{2,1,0:T(8,128)S(1)}, f32[2,256,128]{2,1,0:T(8,128)S(1)}, u32[]{:S(2)}, u32[]{:S(2)}) collective-permute-start(f32[2,256,128]{2,1,0:T(8,128)S(1)} %get-tuple-element.40), channel_id=1, source_target_pairs={{0,16},{16,32},{32,48},{48,64},{64,80},{80,96},{96,112},{112,0},{1... | collective-permute-start | bytes 786440 | tf_op jit(solution)/shard_map/ppermute | solution.py:198
  145.0 116.0 %all-to-all-start.2 = ((f32[8,256,128]{2,1,0:T(8,128)}), f32[8,256,128]{2,1,0:T(8,128)}, u32[]{:S(2)}, u32[]{:S(2)}) async-start(f32[8,256,128]{2,1,0:T(8,128)} %copy-done.7), calls=%async_computation.2 | async-start | bytes 2097152 | tf_op jit(solution)/shard_map/all_to_all | solution.py:471
  150.9 28.0 %collective-permute-start.8 = (f32[1,256,128]{2,1,0:T(8,128)S(1)}, f32[1,256,128]{2,1,0:T(8,128)S(1)}, u32[]{:S(2)}, u32[]{:S(2)}) collective-permute-start(f32[1,256,128]{2,1,0:T(8,128)S(1)} %get-tuple-element.43), channel_id=1, source_target_pairs={{0,112},{16,0},{32,16},{48,32},{64,48},{80,64},{96,80},{112,96},{1... | collective-permute-start | bytes 393224 | tf_op jit(solution)/shard_map/ppermute | solution.py:198
  154.3 33.2 %collective-permute-start.9 = (f32[1,256,128]{2,1,0:T(8,128)S(1)}, f32[1,256,128]{2,1,0:T(8,128)S(1)}, u32[]{:S(2)}, u32[]{:S(2)}) collective-permute-start(f32[1,256,128]{2,1,0:T(8,128)S(1)} %get-tuple-element.44), channel_id=1, source_target_pairs={{0,96},{16,112},{32,0},{48,16},{64,32},{80,48},{96,64},{112,80},{1... | collective-permute-start | bytes 393224 | tf_op jit(solution)/shard_map/ppermute | solution.py:198
  156.6 36.7 %collective-permute-start.10 = (f32[1,256,128]{2,1,0:T(8,128)S(1)}, f32[1,256,128]{2,1,0:T(8,128)S(1)}, u32[]{:S(2)}, u32[]{:S(2)}) collective-permute-start(f32[1,256,128]{2,1,0:T(8,128)S(1)} %get-tuple-element.45), channel_id=1, source_target_pairs={{0,80},{16,96},{32,112},{48,0},{64,16},{80,32},{96,48},{112,64},{1... | collective-permute-start | bytes 393224 | tf_op jit(solution)/shard_map/ppermute | solution.py:198
  158.0 35.2 %collective-permute-start.11 = (f32[1,256,128]{2,1,0:T(8,128)S(1)}, f32[1,256,128]{2,1,0:T(8,128)S(1)}, u32[]{:S(2)}, u32[]{:S(2)}) collective-permute-start(f32[1,256,128]{2,1,0:T(8,128)S(1)} %get-tuple-element.46), channel_id=1, source_target_pairs={{0,64},{16,80},{32,96},{48,112},{64,0},{80,16},{96,32},{112,48},{1... | collective-permute-start | bytes 393224 | tf_op jit(solution)/shard_map/ppermute | solution.py:198
  161.6 31.6 %collective-permute-start.12 = (f32[1,256,128]{2,1,0:T(8,128)S(1)}, f32[1,256,128]{2,1,0:T(8,128)S(1)}, u32[]{:S(2)}, u32[]{:S(2)}) collective-permute-start(f32[1,256,128]{2,1,0:T(8,128)S(1)} %get-tuple-element.47), channel_id=1, source_target_pairs={{0,48},{16,64},{32,80},{48,96},{64,112},{80,0},{96,16},{112,32},{1... | collective-permute-start | bytes 393224 | tf_op jit(solution)/shard_map/ppermute | solution.py:198
  178.8 17.9 %collective-permute-start.13 = (f32[1,256,128]{2,1,0:T(8,128)S(1)}, f32[1,256,128]{2,1,0:T(8,128)S(1)}, u32[]{:S(2)}, u32[]{:S(2)}) collective-permute-start(f32[1,256,128]{2,1,0:T(8,128)S(1)} %get-tuple-element.48), channel_id=1, source_target_pairs={{0,32},{16,48},{32,64},{48,80},{64,96},{80,112},{96,0},{112,16},{1... | collective-permute-start | bytes 393224 | tf_op jit(solution)/shard_map/ppermute | solution.py:198
  187.4 10.8 %collective-permute-start.14 = (f32[1,256,128]{2,1,0:T(8,128)S(1)}, f32[1,256,128]{2,1,0:T(8,128)S(1)}, u32[]{:S(2)}, u32[]{:S(2)}) collective-permute-start(f32[1,256,128]{2,1,0:T(8,128)S(1)} %get-tuple-element.49), channel_id=1, source_target_pairs={{0,16},{16,32},{32,48},{48,64},{64,80},{80,96},{96,112},{112,0},{1... | collective-permute-start | bytes 393224 | tf_op jit(solution)/shard_map/ppermute | solution.py:198
  206.4 12.2 %collective-permute-start.15 = (f32[1,256,128]{2,1,0:T(8,128)S(1)}, f32[1,256,128]{2,1,0:T(8,128)S(1)}, u32[]{:S(2)}, u32[]{:S(2)}) collective-permute-start(f32[1,256,128]{2,1,0:T(8,128)S(1)} %get-tuple-element.51), channel_id=1, source_target_pairs={{0,112},{16,0},{32,16},{48,32},{64,48},{80,64},{96,80},{112,96},{1... | collective-permute-start | bytes 393224 | tf_op jit(solution)/shard_map/ppermute | solution.py:198
  208.0 18.0 %collective-permute-start.16 = (f32[1,256,128]{2,1,0:T(8,128)S(1)}, f32[1,256,128]{2,1,0:T(8,128)S(1)}, u32[]{:S(2)}, u32[]{:S(2)}) collective-permute-start(f32[1,256,128]{2,1,0:T(8,128)S(1)} %get-tuple-element.52), channel_id=1, source_target_pairs={{0,96},{16,112},{32,0},{48,16},{64,32},{80,48},{96,64},{112,80},{1... | collective-permute-start | bytes 393224 | tf_op jit(solution)/shard_map/ppermute | solution.py:198
  210.4 18.0 %collective-permute-start.17 = (f32[1,256,128]{2,1,0:T(8,128)S(1)}, f32[1,256,128]{2,1,0:T(8,128)S(1)}, u32[]{:S(2)}, u32[]{:S(2)}) collective-permute-start(f32[1,256,128]{2,1,0:T(8,128)S(1)} %get-tuple-element.53), channel_id=1, source_target_pairs={{0,80},{16,96},{32,112},{48,0},{64,16},{80,32},{96,48},{112,64},{1... | collective-permute-start | bytes 393224 | tf_op jit(solution)/shard_map/ppermute | solution.py:198
  211.5 16.8 %collective-permute-start.18 = (f32[1,256,128]{2,1,0:T(8,128)S(1)}, f32[1,256,128]{2,1,0:T(8,128)S(1)}, u32[]{:S(2)}, u32[]{:S(2)}) collective-permute-start(f32[1,256,128]{2,1,0:T(8,128)S(1)} %get-tuple-element.54), channel_id=1, source_target_pairs={{0,64},{16,80},{32,96},{48,112},{64,0},{80,16},{96,32},{112,48},{1... | collective-permute-start | bytes 393224 | tf_op jit(solution)/shard_map/ppermute | solution.py:198
  215.3 18.4 %collective-permute-start.19 = (f32[1,256,128]{2,1,0:T(8,128)S(1)}, f32[1,256,128]{2,1,0:T(8,128)S(1)}, u32[]{:S(2)}, u32[]{:S(2)}) collective-permute-start(f32[1,256,128]{2,1,0:T(8,128)S(1)} %get-tuple-element.55), channel_id=1, source_target_pairs={{0,48},{16,64},{32,80},{48,96},{64,112},{80,0},{96,16},{112,32},{1... | collective-permute-start | bytes 393224 | tf_op jit(solution)/shard_map/ppermute | solution.py:198
  218.6 16.2 %collective-permute-start.20 = (f32[1,256,128]{2,1,0:T(8,128)S(1)}, f32[1,256,128]{2,1,0:T(8,128)S(1)}, u32[]{:S(2)}, u32[]{:S(2)}) collective-permute-start(f32[1,256,128]{2,1,0:T(8,128)S(1)} %get-tuple-element.56), channel_id=1, source_target_pairs={{0,32},{16,48},{32,64},{48,80},{64,96},{80,112},{96,0},{112,16},{1... | collective-permute-start | bytes 393224 | tf_op jit(solution)/shard_map/ppermute | solution.py:198
  226.0 12.9 %collective-permute-start.21 = (f32[1,256,128]{2,1,0:T(8,128)S(1)}, f32[1,256,128]{2,1,0:T(8,128)S(1)}, u32[]{:S(2)}, u32[]{:S(2)}) collective-permute-start(f32[1,256,128]{2,1,0:T(8,128)S(1)} %get-tuple-element.57), channel_id=1, source_target_pairs={{0,16},{16,32},{32,48},{48,64},{64,80},{80,96},{96,112},{112,0},{1... | collective-permute-start | bytes 393224 | tf_op jit(solution)/shard_map/ppermute | solution.py:198
  245.4 5.1 %collective-permute-start.23 = (f32[8,128]{1,0:T(8,128)S(1)}, f32[8,128]{1,0:T(8,128)S(1)}, u32[]{:S(2)}, u32[]{:S(2)}) collective-permute-start(f32[8,128]{1,0:T(8,128)S(1)} %get-tuple-element.62), channel_id=1, source_target_pairs={{0,2},{1,3},{2,0},{3,1},{4,6},{5,7},{6,4},{7,5},{8,10},{9,11},{10,... | collective-permute-start | bytes 12296 | tf_op jit(solution)/shard_map/ppermute | solution.py:493
  250.5 5.1 %collective-permute-start.27 = (f32[8,128]{1,0:T(8,128)S(1)}, f32[8,128]{1,0:T(8,128)S(1)}, u32[]{:S(2)}, u32[]{:S(2)}) collective-permute-start(f32[8,128]{1,0:T(8,128)S(1)} %add_add_fusion.3), channel_id=1, source_target_pairs={{0,4},{4,8},{8,12},{12,0},{1,5},{5,9},{9,13},{13,1},{2,6},{6,10},{... | collective-permute-start | bytes 12296 | tf_op jit(solution)/shard_map/ppermute | solution.py:493
  253.7 5.1 %collective-permute-start.26 = (f32[8,128]{1,0:T(8,128)S(1)}, f32[8,128]{1,0:T(8,128)S(1)}, u32[]{:S(2)}, u32[]{:S(2)}) collective-permute-start(f32[8,128]{1,0:T(8,128)S(1)} %add_add_fusion.3), channel_id=1, source_target_pairs={{0,8},{4,12},{8,0},{12,4},{1,9},{5,13},{9,1},{13,5},{2,10},{6,14},... | collective-permute-start | bytes 12296 | tf_op jit(solution)/shard_map/ppermute | solution.py:493
  258.8 5.8 %collective-permute-start.30 = (f32[8,128]{1,0:T(8,128)S(1)}, f32[8,128]{1,0:T(8,128)S(1)}, u32[]{:S(2)}, u32[]{:S(2)}) collective-permute-start(f32[8,128]{1,0:T(8,128)S(1)} %add_add_fusion.2), channel_id=1, source_target_pairs={{0,16},{16,0},{32,48},{48,32},{64,80},{80,64},{96,112},{112,96},{1... | collective-permute-start | bytes 12296 | tf_op jit(solution)/shard_map/ppermute | solution.py:493
  264.6 8.0 %collective-permute-start.22 = (f32[16,128]{1,0:T(8,128)S(1)}, f32[16,128]{1,0:T(8,128)S(1)}, u32[]{:S(2)}, u32[]{:S(2)}) collective-permute-start(f32[16,128]{1,0:T(8,128)S(1)} %get-tuple-element.61), channel_id=1, source_target_pairs={{0,128},{128,0},{1,129},{129,1},{2,130},{130,2},{3,131},{131,3},{4... | collective-permute-start | bytes 24584 | tf_op jit(solution)/shard_map/ppermute | solution.py:487
  264.6 8.6 %collective-permute-start.33 = (f32[8,128]{1,0:T(8,128)S(1)}, f32[8,128]{1,0:T(8,128)S(1)}, u32[]{:S(2)}, u32[]{:S(2)}) collective-permute-start(f32[8,128]{1,0:T(8,128)S(1)} %add_add_fusion.1), channel_id=1, source_target_pairs={{0,32},{16,48},{32,64},{48,80},{64,96},{80,112},{96,0},{112,16},{1... | collective-permute-start | bytes 12296 | tf_op jit(solution)/shard_map/ppermute | solution.py:493
  265.6 7.6 %collective-permute-start.34 = (f32[8,128]{1,0:T(8,128)S(1)}, f32[8,128]{1,0:T(8,128)S(1)}, u32[]{:S(2)}, u32[]{:S(2)}) collective-permute-start(f32[8,128]{1,0:T(8,128)S(1)} %add_add_fusion.1), channel_id=1, source_target_pairs={{0,96},{16,112},{32,0},{48,16},{64,32},{80,48},{96,64},{112,80},{1... | collective-permute-start | bytes 12296 | tf_op jit(solution)/shard_map/ppermute | solution.py:493
  268.8 7.5 %collective-permute-start.32 = (f32[8,128]{1,0:T(8,128)S(1)}, f32[8,128]{1,0:T(8,128)S(1)}, u32[]{:S(2)}, u32[]{:S(2)}) collective-permute-start(f32[8,128]{1,0:T(8,128)S(1)} %add_add_fusion.1), channel_id=1, source_target_pairs={{0,64},{16,80},{32,96},{48,112},{64,0},{80,16},{96,32},{112,48},{1... | collective-permute-start | bytes 12296 | tf_op jit(solution)/shard_map/ppermute | solution.py:493
  (15 other events, 194.9 us)
where the time goes:
time: 278 us; the launch traced here: 277 us
  waiting for transfers between devices  150 us (54%)
  starting transfers between devices  77 us (28%)
  Pallas kernels  41 us (15%)
  local copies, waits for them, and re-layouts  8.04 us (3%)
    ppermute x21, waiting for transfers between devices, send_blocks(): got[(ROWS - dist) % ROWS] = lax.ppermute(blocks[dist], 'row', perm)  100 us
    ppermute x21, starting transfers between devices, send_blocks(): got[(ROWS - dist) % ROWS] = lax.ppermute(blocks[dist], 'row', perm)  38.6 us
    all_to_all x1, waiting for transfers between devices, whole_step(): lax.all_to_all(for_cols, PLANE_COL, split_axis=0, concat_axis=0, tiled=True)  37.9 us
    pallas_call x7, Pallas kernels, call(): pl.pallas_call(kernel, out_shape=list(outs) if many else outs, in_specs=s...  36.8 us
    ppermute x12, starting transfers between devices, sum_of_four(): lax.ppermute(values, axis, [(i, partner(i, n)) for i in range(size)])  19.3 us
    ppermute x12, waiting for transfers between devices, sum_of_four(): lax.ppermute(values, axis, [(i, partner(i, n)) for i in range(size)])  9.47 us
    all_to_all x1, starting transfers between devices, whole_step(): lax.all_to_all(for_cols, PLANE_COL, split_axis=0, concat_axis=0, tiled=True)  7.75 us
    unnamed x19, local copies, waits for them, and re-layouts  7.46 us
  transfers between devices with their start and end apart: 38, of which 21 were waited for; matrix products, arithmetic and copies ran while one was open for 0% of the time, Pallas kernels for 11%

commit v1 on v0

--- a/solution.py
+++ b/solution.py
@@ -71,6 +71,14 @@
 
 def near(values):
     return pltpu.with_memory_space_constraint(values, pltpu.VMEM)
+
+
+def far(values):
+    return pltpu.with_memory_space_constraint(values, pltpu.HBM)
+
+
+def f32_far(*shape):
+    return pltpu.HBM(shape, jnp.float32)
 
 
 def f32(*shape):
@@ -171,7 +179,7 @@
 
     return pl.pallas_call(
         functools.partial(pack_rows_kernel, count=count),
-        out_shape=[f32(count, 256, 128)] * ROWS,
+        out_shape=[f32_far(count, 256, 128)] * ROWS,
         grid=(1,),
         in_specs=[pl.BlockSpec(memory_space=pltpu.SMEM)] + [one(c) for c in comps],
         out_specs=[whole] * ROWS,
@@ -192,7 +200,7 @@
 
 
 def send_blocks(blocks):
-    got = [blocks[0]] + [None] * (ROWS - 1)
+    got = [far(blocks[0])] + [None] * (ROWS - 1)
     for dist in DISTANCES:
         perm = [(i, (i + dist) % ROWS) for i in range(ROWS)]
         got[(ROWS - dist) % ROWS] = lax.ppermute(blocks[dist], "row", perm)
@@ -258,7 +266,7 @@
 
 
 def grad_v(tables, blocks):
-    return vmem_call(grad_v_kernel, [f32(1, 256, 128)] * 8, X_SCRATCH)(*tables, *blocks)
+    return vmem_call(grad_v_kernel, [f32_far(1, 256, 128)] * 8, X_SCRATCH)(*tables, *blocks)
 
 
 def stack_first_kernel(*refs):
@@ -471,7 +479,7 @@
     x_terms = lax.all_to_all(x_terms, "row", split_axis=0, concat_axis=0, tiled=True)
     held = pltpu.VMEM((ROWS, 256, 128), jnp.float32)
     place = jnp.stack([row, col]).astype(jnp.int32)
-    part, coarse = vmem_call(partial_kernel, [f32(2, 512, 256), f32(8, 128)], (held,), smem=1)(
+    part, coarse = vmem_call(partial_kernel, [f32_far(2, 512, 256), f32(8, 128)], (held,), smem=1)(
         place, near(y_terms), x_sums, *v_x
     )
     coarse = sum_of_four(coarse, "col_1", lambda i, n: (i + (2, 1, 3)[n]) % 4)
@@ -483,7 +491,7 @@
         final_kernel,
         [f32(2, 512, 256), f32(16, 128)],
         (pltpu.VMEM((16, 8, 256), jnp.float32),),
-    )(part, near(x_terms))
+    )(far(part), near(x_terms))
     fine = (fine + lax.ppermute(fine, "plane", [(0, 1), (1, 0)]))[:, :8]
     return dissip, fine, coarse
 

time: 278 us -> 285 us (1.025)
  Pallas kernels: 41 us -> 48.2 us
    pallas_call x7, Pallas kernels: 36.8 us -> 40.9 us  [call(): pl.pallas_call(kernel, out_shape=list(outs) if many else outs, in_specs=s...]
  transfers between devices with their start and end apart: 38 -> 38, of which waited for: 21 -> 21; matrix products, arithmetic and copies ran while one was open for 0% -> 0% of each run, Pallas kernels for 11% -> 13%
where the time goes in v1:
time: 285 us; the launch traced here: 283 us
  waiting for transfers between devices  150 us (53%)
  starting transfers between devices  76.4 us (27%)
  Pallas kernels  48.2 us (17%)
  local copies, waits for them, and re-layouts  8.04 us (3%)
    ppermute x21, waiting for transfers between devices, send_blocks(): got[(ROWS - dist) % ROWS] = lax.ppermute(blocks[dist], 'row', perm)  99.6 us
    pallas_call x7, Pallas kernels, call(): pl.pallas_call(kernel, out_shape=list(outs) if many else outs, in_specs=s...  40.9 us
    ppermute x21, starting transfers between devices, send_blocks(): got[(ROWS - dist) % ROWS] = lax.ppermute(blocks[dist], 'row', perm)  38.2 us
    all_to_all x1, waiting for transfers between devices, whole_step(): lax.all_to_all(for_cols, PLANE_COL, split_axis=0, concat_axis=0, tiled=True)  37.9 us
    ppermute x12, starting transfers between devices, sum_of_four(): lax.ppermute(values, axis, [(i, partner(i, n)) for i in range(size)])  19.1 us
    ppermute x12, waiting for transfers between devices, sum_of_four(): lax.ppermute(values, axis, [(i, partner(i, n)) for i in range(size)])  9.55 us
    all_to_all x1, starting transfers between devices, whole_step(): lax.all_to_all(for_cols, PLANE_COL, split_axis=0, concat_axis=0, tiled=True)  7.75 us
    unnamed x19, local copies, waits for them, and re-layouts  7.46 us
  transfers between devices with their start and end apart: 38, of which 21 were waited for; matrix products, arithmetic and copies ran while one was open for 0% of the time, Pallas kernels for 13%

profile of v1, /device:TPU:2, one launch (start us, length us, event | category | flops | bytes accessed | tf_op | source)
XLA Modules:
  0.0 283.4 jit_solution(14161618118245429089)
XLA Ops:
  4.4 7.7 %all-to-all-start = ((f32[32,3,2,16,256]{4,3,2,1,0:T(8,128)}), f32[32,3,2,16,256]{4,3,2,1,0:T(8,128)S(1)}, u32[]{:S(2)}, u32[]{:S(2)}) async-start(f32[32,3,2,16,256]{4,3,2,1,0:T(8,128)} %copy-done.2), calls=%async_computation | async-start | bytes 6291456 | tf_op jit(solution)/shard_map/all_to_all | solution.py:464
  13.2 37.9 %all-to-all-done = f32[32,3,2,16,256]{4,3,2,1,0:T(8,128)S(1)} async-done(((f32[32,3,2,16,256]{4,3,2,1,0:T(8,128)}), f32[32,3,2,16,256]{4,3,2,1,0:T(8,128)S(1)}, u32[]{:S(2)}, u32[]{:S(2)}) %all-to-all-start) | async-done | bytes 3145760 | tf_op jit(solution)/shard_map/all_to_all | solution.py:464
  52.1 10.1 %shard_map.60 = f32[2,16,2,2,16,256]{5,4,3,2,1,0:T(8,128)S(1)} custom-call(f32[256,256]{1,0:T(8,128)S(1)} %shard_map.58.base.refs_0_, f32[16,2,1,256]{3,2,1,0:T(1,128)S(1)} %copy-done.8, f32[2,256,128]{2,1,0:T(8,128)S(1)} %copy-done.4, f32[2,16,3,2,16,256]{5,4,3,2,1,0:T(8,128)S(1)} %bitcast.4), custom_call_target="tpu_custom_call" | custom-call | tf_op jit(solution)/shard_map/pallas_call | solution.py:60
  63.6 7.0 %all-to-all-start.1 = ((f32[32,2,2,16,256]{4,3,2,1,0:T(8,128)}), f32[32,2,2,16,256]{4,3,2,1,0:T(8,128)}, u32[]{:S(2)}, u32[]{:S(2)}) async-start(f32[32,2,2,16,256]{4,3,2,1,0:T(8,128)} %bitcast.5), calls=%async_computation.1 | async-start | bytes 4194304 | tf_op jit(solution)/shard_map/all_to_all | solution.py:473
  70.6 3.8 %pack_rows.2 = (f32[2,256,128]{2,1,0:T(8,128)}, f32[2,256,128]{2,1,0:T(8,128)}, f32[2,256,128]{2,1,0:T(8,128)}, f32[2,256,128]{2,1,0:T(8,128)}, f32[2,256,128]{2...) custom-call(s32[1]{0:T(128)} %bitcast.row, ...), custom_call_target="tpu_custom_call" | custom-call | tf_op jit(solution)/shard_map/pack_rows/pallas_call | solution.py:180
  74.4 5.9 %collective-permute-start = (f32[2,256,128]{2,1,0:T(8,128)}, f32[2,256,128]{2,1,0:T(8,128)S(1)}, u32[]{:S(2)}, u32[]{:S(2)}) collective-permute-start(f32[2,256,128]{2,1,0:T(8,128)} %get-tuple-element.34), channel_id=1, source_target_pairs={{0,112},{16,0},{32,16},{48,32},{64,48},{80,64},{96,80},{112,96},{1... | collective-permute-start | bytes 786440 | tf_op jit(solution)/shard_map/ppermute | solution.py:206
  82.1 5.0 %collective-permute-start.3 = (f32[2,256,128]{2,1,0:T(8,128)}, f32[2,256,128]{2,1,0:T(8,128)S(1)}, u32[]{:S(2)}, u32[]{:S(2)}) collective-permute-start(f32[2,256,128]{2,1,0:T(8,128)} %get-tuple-element.37), channel_id=1, source_target_pairs={{0,64},{16,80},{32,96},{48,112},{64,0},{80,16},{96,32},{112,48},{1... | collective-permute-start | bytes 786440 | tf_op jit(solution)/shard_map/ppermute | solution.py:206
  87.2 6.8 %collective-permute-done.refs_1_.refs_4_ = f32[2,256,128]{2,1,0:T(8,128)S(1)} collective-permute-done((f32[2,256,128]{2,1,0:T(8,128)}, f32[2,256,128]{2,1,0:T(8,128)S(1)}, u32[]{:S(2)}, u32[]{:S(2)}) %collective-permute-start) | collective-permute-done | bytes 262176 | tf_op jit(solution)/shard_map/ppermute | solution.py:206
  93.9 12.7 %collective-permute-done.1.refs_2_.refs_5_ = f32[2,256,128]{2,1,0:T(8,128)S(1)} collective-permute-done((f32[2,256,128]{2,1,0:T(8,128)}, f32[2,256,128]{2,1,0:T(8,128)S(1)}, u32[]{:S(2)}, u32[]{:S(2)}) %collective-permute-start.1) | collective-permute-done | bytes 262176 | tf_op jit(solution)/shard_map/ppermute | solution.py:206
  106.6 19.2 %collective-permute-done.2.refs_3_.refs_6_ = f32[2,256,128]{2,1,0:T(8,128)S(1)} collective-permute-done((f32[2,256,128]{2,1,0:T(8,128)}, f32[2,256,128]{2,1,0:T(8,128)S(1)}, u32[]{:S(2)}, u32[]{:S(2)}) %collective-permute-start.2) | collective-permute-done | bytes 262176 | tf_op jit(solution)/shard_map/ppermute | solution.py:206
  125.8 3.8 %collective-permute-done.5.refs_6_.refs_9_ = f32[2,256,128]{2,1,0:T(8,128)S(1)} collective-permute-done((f32[2,256,128]{2,1,0:T(8,128)}, f32[2,256,128]{2,1,0:T(8,128)S(1)}, u32[]{:S(2)}, u32[]{:S(2)}) %collective-permute-start.5) | collective-permute-done | bytes 262176 | tf_op jit(solution)/shard_map/ppermute | solution.py:206
  129.6 3.7 %collective-permute-done.6.refs_7_.refs_10_ = f32[2,256,128]{2,1,0:T(8,128)S(1)} collective-permute-done((f32[2,256,128]{2,1,0:T(8,128)}, f32[2,256,128]{2,1,0:T(8,128)S(1)}, u32[]{:S(2)}, u32[]{:S(2)}) %collective-permute-start.6) | collective-permute-done | bytes 262176 | tf_op jit(solution)/shard_map/ppermute | solution.py:206
  137.0 10.2 %shard_map.61 = (f32[8,256,128]{2,1,0:T(8,128)S(1)}, f32[8,128]{1,0:T(8,128)S(1)}) custom-call(s32[1]{0:T(128)} %bitcast.row, f32[256,256]{1,0:T(8,128)S(1)} %shard_map.58.base.refs_0_, f32[16,2,1,256]{3,2,1,0:T(1,128)S(1)} %copy-done.8, f32[2,256,128]{2,1,0:T(8,128)S(1)} %copy-done.5, f32[2,256,128]{2,1,0:T(8,128)} %get-tuple-element.33.refs_0_.refs_3_, ...), custom_call_target="tpu_custom_call" | custom-call | tf_op jit(solution)/shard_map/pallas_call | solution.py:60
  148.3 4.2 %all-to-all-start.2 = ((f32[8,256,128]{2,1,0:T(8,128)}), f32[8,256,128]{2,1,0:T(8,128)}, u32[]{:S(2)}, u32[]{:S(2)}) async-start(f32[8,256,128]{2,1,0:T(8,128)} %copy-done.7), calls=%async_computation.2 | async-start | bytes 2097152 | tf_op jit(solution)/shard_map/all_to_all | solution.py:479
  155.2 3.1 %collective-permute-start.8 = (f32[1,256,128]{2,1,0:T(8,128)}, f32[1,256,128]{2,1,0:T(8,128)S(1)}, u32[]{:S(2)}, u32[]{:S(2)}) collective-permute-start(f32[1,256,128]{2,1,0:T(8,128)} %get-tuple-element.43), channel_id=1, source_target_pairs={{0,112},{16,0},{32,16},{48,32},{64,48},{80,64},{96,80},{112,96},{1... | collective-permute-start | bytes 393224 | tf_op jit(solution)/shard_map/ppermute | solution.py:206
  162.1 3.6 %collective-permute-start.11 = (f32[1,256,128]{2,1,0:T(8,128)}, f32[1,256,128]{2,1,0:T(8,128)S(1)}, u32[]{:S(2)}, u32[]{:S(2)}) collective-permute-start(f32[1,256,128]{2,1,0:T(8,128)} %get-tuple-element.46), channel_id=1, source_target_pairs={{0,64},{16,80},{32,96},{48,112},{64,0},{80,16},{96,32},{112,48},{1... | collective-permute-start | bytes 393224 | tf_op jit(solution)/shard_map/ppermute | solution.py:206
  165.9 16.2 %collective-permute-done.8.refs_4_ = f32[1,256,128]{2,1,0:T(8,128)S(1)} collective-permute-done((f32[1,256,128]{2,1,0:T(8,128)}, f32[1,256,128]{2,1,0:T(8,128)S(1)}, u32[]{:S(2)}, u32[]{:S(2)}) %collective-permute-start.8) | collective-permute-done | bytes 131104 | tf_op jit(solution)/shard_map/ppermute | solution.py:206
  183.8 6.9 %collective-permute-done.9.refs_5_ = f32[1,256,128]{2,1,0:T(8,128)S(1)} collective-permute-done((f32[1,256,128]{2,1,0:T(8,128)}, f32[1,256,128]{2,1,0:T(8,128)S(1)}, u32[]{:S(2)}, u32[]{:S(2)}) %collective-permute-start.9) | collective-permute-done | bytes 131104 | tf_op jit(solution)/shard_map/ppermute | solution.py:206
  190.7 5.9 %collective-permute-done.10.refs_6_ = f32[1,256,128]{2,1,0:T(8,128)S(1)} collective-permute-done((f32[1,256,128]{2,1,0:T(8,128)}, f32[1,256,128]{2,1,0:T(8,128)S(1)}, u32[]{:S(2)}, u32[]{:S(2)}) %collective-permute-start.10) | collective-permute-done | bytes 131104 | tf_op jit(solution)/shard_map/ppermute | solution.py:206
  196.5 3.5 %collective-permute-done.13.refs_9_ = f32[1,256,128]{2,1,0:T(8,128)S(1)} collective-permute-done((f32[1,256,128]{2,1,0:T(8,128)}, f32[1,256,128]{2,1,0:T(8,128)S(1)}, u32[]{:S(2)}, u32[]{:S(2)}) %collective-permute-start.13) | collective-permute-done | bytes 131104 | tf_op jit(solution)/shard_map/ppermute | solution.py:206
  201.5 10.0 %shard_map.62 = (f32[1,256,128]{2,1,0:T(8,128)}, f32[1,256,128]{2,1,0:T(8,128)}, f32[1,256,128]{2,1,0:T(8,128)}, f32[1,256,128]{2,1,0:T(8,128)}, f32[1,256,128]{...) custom-call(f32[256,256]{1,0:T(8,128)S(1)} %shard_map.58.base.refs_0_, ...), custom_call_target="tpu_custom_call" | custom-call | tf_op jit(solution)/shard_map/pallas_call | solution.py:60
  216.5 3.9 %collective-permute-start.18 = (f32[1,256,128]{2,1,0:T(8,128)}, f32[1,256,128]{2,1,0:T(8,128)S(1)}, u32[]{:S(2)}, u32[]{:S(2)}) collective-permute-start(f32[1,256,128]{2,1,0:T(8,128)} %get-tuple-element.54), channel_id=1, source_target_pairs={{0,64},{16,80},{32,96},{48,112},{64,0},{80,16},{96,32},{112,48},{1... | collective-permute-start | bytes 393224 | tf_op jit(solution)/shard_map/ppermute | solution.py:206
  220.4 3.3 %collective-permute-start.19 = (f32[1,256,128]{2,1,0:T(8,128)}, f32[1,256,128]{2,1,0:T(8,128)S(1)}, u32[]{:S(2)}, u32[]{:S(2)}) collective-permute-start(f32[1,256,128]{2,1,0:T(8,128)} %get-tuple-element.55), channel_id=1, source_target_pairs={{0,48},{16,64},{32,80},{48,96},{64,112},{80,0},{96,16},{112,32},{1... | collective-permute-start | bytes 393224 | tf_op jit(solution)/shard_map/ppermute | solution.py:206
  224.5 6.6 %collective-permute-done.16.refs_2_ = f32[1,256,128]{2,1,0:T(8,128)S(1)} collective-permute-done((f32[1,256,128]{2,1,0:T(8,128)}, f32[1,256,128]{2,1,0:T(8,128)S(1)}, u32[]{:S(2)}, u32[]{:S(2)}) %collective-permute-start.16) | collective-permute-done | bytes 131104 | tf_op jit(solution)/shard_map/ppermute | solution.py:206
  233.3 5.6 %collective-permute-done.19.refs_5_ = f32[1,256,128]{2,1,0:T(8,128)S(1)} collective-permute-done((f32[1,256,128]{2,1,0:T(8,128)}, f32[1,256,128]{2,1,0:T(8,128)S(1)}, u32[]{:S(2)}, u32[]{:S(2)}) %collective-permute-start.19) | collective-permute-done | bytes 131104 | tf_op jit(solution)/shard_map/ppermute | solution.py:206
  240.2 3.9 %collective-permute-done.21.refs_7_ = f32[1,256,128]{2,1,0:T(8,128)S(1)} collective-permute-done((f32[1,256,128]{2,1,0:T(8,128)}, f32[1,256,128]{2,1,0:T(8,128)S(1)}, u32[]{:S(2)}, u32[]{:S(2)}) %collective-permute-start.21) | collective-permute-done | bytes 131104 | tf_op jit(solution)/shard_map/ppermute | solution.py:206
  244.1 5.3 %shard_map.63 = (f32[2,512,256]{2,1,0:T(8,128)}, f32[8,128]{1,0:T(8,128)S(1)}) custom-call(s32[2]{0:T(128)S(1)} %pad_add_fusion.place, f32[32,2,2,16,256]{4,3,2,1,0:T(8,128)} %all-to-all-done.1.y_terms, f32[8,128]{1,0:T(8,128)S(1)} %get-tuple-element.41.x_sums, f32[1,256,128]{2,1,0:T(8,128)} %get-tuple-element.50.refs_0_, ...), custom_call_target="tpu_custom_call" | custom-call | tf_op jit(solution)/shard_map/pallas_call | solution.py:60
  261.7 3.2 %collective-permute-done.26 = f32[8,128]{1,0:T(8,128)S(1)} collective-permute-done((f32[8,128]{1,0:T(8,128)S(1)}, f32[8,128]{1,0:T(8,128)S(1)}, u32[]{:S(2)}, u32[]{:S(2)}) %collective-permute-start.26) | collective-permute-done | bytes 4128 | tf_op jit(solution)/shard_map/ppermute | solution.py:501
  267.1 3.9 %shard_map.64 = (f32[2,512,256]{2,1,0:T(8,128)}, f32[16,128]{1,0:T(8,128)S(1)}) custom-call(f32[2,512,256]{2,1,0:T(8,128)} %get-tuple-element.58.part, f32[8,256,128]{2,1,0:T(8,128)} %all-to-all-done.2.held), custom_call_target="tpu_custom_call" | custom-call | tf_op jit(solution)/shard_map/pallas_call | solution.py:60
  272.0 3.2 %collective-permute-start.34 = (f32[8,128]{1,0:T(8,128)S(1)}, f32[8,128]{1,0:T(8,128)S(1)}, u32[]{:S(2)}, u32[]{:S(2)}) collective-permute-start(f32[8,128]{1,0:T(8,128)S(1)} %add_add_fusion.1), channel_id=1, source_target_pairs={{0,96},{16,112},{32,0},{48,16},{64,32},{80,48},{96,64},{112,80},{1... | collective-permute-start | bytes 12296 | tf_op jit(solution)/shard_map/ppermute | solution.py:501
  275.3 3.6 %collective-permute-start.32 = (f32[8,128]{1,0:T(8,128)S(1)}, f32[8,128]{1,0:T(8,128)S(1)}, u32[]{:S(2)}, u32[]{:S(2)}) collective-permute-start(f32[8,128]{1,0:T(8,128)S(1)} %add_add_fusion.1), channel_id=1, source_target_pairs={{0,64},{16,80},{32,96},{48,112},{64,0},{80,16},{96,32},{112,48},{1... | collective-permute-start | bytes 12296 | tf_op jit(solution)/shard_map/ppermute | solution.py:501
  279.6 3.2 %collective-permute-done.32 = f32[8,128]{1,0:T(8,128)S(1)} collective-permute-done((f32[8,128]{1,0:T(8,128)S(1)}, f32[8,128]{1,0:T(8,128)S(1)}, u32[]{:S(2)}, u32[]{:S(2)}) %collective-permute-start.32) | collective-permute-done | bytes 4128 | tf_op jit(solution)/shard_map/ppermute | solution.py:501
  (80 shorter events, 49.5 us)
Async XLA Ops:
  4.4 46.7 %all-to-all-start = ((f32[32,3,2,16,256]{4,3,2,1,0:T(8,128)}), f32[32,3,2,16,256]{4,3,2,1,0:T(8,128)S(1)}, u32[]{:S(2)}, u32[]{:S(2)}) async-start(f32[32,3,2,16,256]{4,3,2,1,0:T(8,128)} %copy-done.2), calls=%async_computation | async-start | bytes 6291456 | tf_op jit(solution)/shard_map/all_to_all | solution.py:464
  63.6 84.7 %all-to-all-start.1 = ((f32[32,2,2,16,256]{4,3,2,1,0:T(8,128)}), f32[32,2,2,16,256]{4,3,2,1,0:T(8,128)}, u32[]{:S(2)}, u32[]{:S(2)}) async-start(f32[32,2,2,16,256]{4,3,2,1,0:T(8,128)} %bitcast.5), calls=%async_computation.1 | async-start | bytes 4194304 | tf_op jit(solution)/shard_map/all_to_all | solution.py:473
  74.4 19.6 %collective-permute-start = (f32[2,256,128]{2,1,0:T(8,128)}, f32[2,256,128]{2,1,0:T(8,128)S(1)}, u32[]{:S(2)}, u32[]{:S(2)}) collective-permute-start(f32[2,256,128]{2,1,0:T(8,128)} %get-tuple-element.34), channel_id=1, source_target_pairs={{0,112},{16,0},{32,16},{48,32},{64,48},{80,64},{96,80},{112,96},{1... | collective-permute-start | bytes 786440 | tf_op jit(solution)/shard_map/ppermute | solution.py:206
  80.2 26.4 %collective-permute-start.1 = (f32[2,256,128]{2,1,0:T(8,128)}, f32[2,256,128]{2,1,0:T(8,128)S(1)}, u32[]{:S(2)}, u32[]{:S(2)}) collective-permute-start(f32[2,256,128]{2,1,0:T(8,128)} %get-tuple-element.35), channel_id=1, source_target_pairs={{0,96},{16,112},{32,0},{48,16},{64,32},{80,48},{96,64},{112,80},{1... | collective-permute-start | bytes 786440 | tf_op jit(solution)/shard_map/ppermute | solution.py:206
  81.7 44.1 %collective-permute-start.2 = (f32[2,256,128]{2,1,0:T(8,128)}, f32[2,256,128]{2,1,0:T(8,128)S(1)}, u32[]{:S(2)}, u32[]{:S(2)}) collective-permute-start(f32[2,256,128]{2,1,0:T(8,128)} %get-tuple-element.36), channel_id=1, source_target_pairs={{0,80},{16,96},{32,112},{48,0},{64,16},{80,32},{96,48},{112,64},{1... | collective-permute-start | bytes 786440 | tf_op jit(solution)/shard_map/ppermute | solution.py:206
  82.1 43.7 %collective-permute-start.3 = (f32[2,256,128]{2,1,0:T(8,128)}, f32[2,256,128]{2,1,0:T(8,128)S(1)}, u32[]{:S(2)}, u32[]{:S(2)}) collective-permute-start(f32[2,256,128]{2,1,0:T(8,128)} %get-tuple-element.37), channel_id=1, source_target_pairs={{0,64},{16,80},{32,96},{48,112},{64,0},{80,16},{96,32},{112,48},{1... | collective-permute-start | bytes 786440 | tf_op jit(solution)/shard_map/ppermute | solution.py:206
  87.2 38.7 %collective-permute-start.4 = (f32[2,256,128]{2,1,0:T(8,128)}, f32[2,256,128]{2,1,0:T(8,128)S(1)}, u32[]{:S(2)}, u32[]{:S(2)}) collective-permute-start(f32[2,256,128]{2,1,0:T(8,128)} %get-tuple-element.38), channel_id=1, source_target_pairs={{0,48},{16,64},{32,80},{48,96},{64,112},{80,0},{96,16},{112,32},{1... | collective-permute-start | bytes 786440 | tf_op jit(solution)/shard_map/ppermute | solution.py:206
  93.9 35.7 %collective-permute-start.5 = (f32[2,256,128]{2,1,0:T(8,128)}, f32[2,256,128]{2,1,0:T(8,128)S(1)}, u32[]{:S(2)}, u32[]{:S(2)}) collective-permute-start(f32[2,256,128]{2,1,0:T(8,128)} %get-tuple-element.39), channel_id=1, source_target_pairs={{0,32},{16,48},{32,64},{48,80},{64,96},{80,112},{96,0},{112,16},{1... | collective-permute-start | bytes 786440 | tf_op jit(solution)/shard_map/ppermute | solution.py:206
  106.6 26.7 %collective-permute-start.6 = (f32[2,256,128]{2,1,0:T(8,128)}, f32[2,256,128]{2,1,0:T(8,128)S(1)}, u32[]{:S(2)}, u32[]{:S(2)}) collective-permute-start(f32[2,256,128]{2,1,0:T(8,128)} %get-tuple-element.40), channel_id=1, source_target_pairs={{0,16},{16,32},{32,48},{48,64},{64,80},{80,96},{96,112},{112,0},{1... | collective-permute-start | bytes 786440 | tf_op jit(solution)/shard_map/ppermute | solution.py:206
  148.3 118.8 %all-to-all-start.2 = ((f32[8,256,128]{2,1,0:T(8,128)}), f32[8,256,128]{2,1,0:T(8,128)}, u32[]{:S(2)}, u32[]{:S(2)}) async-start(f32[8,256,128]{2,1,0:T(8,128)} %copy-done.7), calls=%async_computation.2 | async-start | bytes 2097152 | tf_op jit(solution)/shard_map/all_to_all | solution.py:479
  155.2 26.9 %collective-permute-start.8 = (f32[1,256,128]{2,1,0:T(8,128)}, f32[1,256,128]{2,1,0:T(8,128)S(1)}, u32[]{:S(2)}, u32[]{:S(2)}) collective-permute-start(f32[1,256,128]{2,1,0:T(8,128)} %get-tuple-element.43), channel_id=1, source_target_pairs={{0,112},{16,0},{32,16},{48,32},{64,48},{80,64},{96,80},{112,96},{1... | collective-permute-start | bytes 393224 | tf_op jit(solution)/shard_map/ppermute | solution.py:206
  158.3 32.4 %collective-permute-start.9 = (f32[1,256,128]{2,1,0:T(8,128)}, f32[1,256,128]{2,1,0:T(8,128)S(1)}, u32[]{:S(2)}, u32[]{:S(2)}) collective-permute-start(f32[1,256,128]{2,1,0:T(8,128)} %get-tuple-element.44), channel_id=1, source_target_pairs={{0,96},{16,112},{32,0},{48,16},{64,32},{80,48},{96,64},{112,80},{1... | collective-permute-start | bytes 393224 | tf_op jit(solution)/shard_map/ppermute | solution.py:206
  160.6 35.9 %collective-permute-start.10 = (f32[1,256,128]{2,1,0:T(8,128)}, f32[1,256,128]{2,1,0:T(8,128)S(1)}, u32[]{:S(2)}, u32[]{:S(2)}) collective-permute-start(f32[1,256,128]{2,1,0:T(8,128)} %get-tuple-element.45), channel_id=1, source_target_pairs={{0,80},{16,96},{32,112},{48,0},{64,16},{80,32},{96,48},{112,64},{1... | collective-permute-start | bytes 393224 | tf_op jit(solution)/shard_map/ppermute | solution.py:206
  162.1 34.5 %collective-permute-start.11 = (f32[1,256,128]{2,1,0:T(8,128)}, f32[1,256,128]{2,1,0:T(8,128)S(1)}, u32[]{:S(2)}, u32[]{:S(2)}) collective-permute-start(f32[1,256,128]{2,1,0:T(8,128)} %get-tuple-element.46), channel_id=1, source_target_pairs={{0,64},{16,80},{32,96},{48,112},{64,0},{80,16},{96,32},{112,48},{1... | collective-permute-start | bytes 393224 | tf_op jit(solution)/shard_map/ppermute | solution.py:206
  165.7 30.9 %collective-permute-start.12 = (f32[1,256,128]{2,1,0:T(8,128)}, f32[1,256,128]{2,1,0:T(8,128)S(1)}, u32[]{:S(2)}, u32[]{:S(2)}) collective-permute-start(f32[1,256,128]{2,1,0:T(8,128)} %get-tuple-element.47), channel_id=1, source_target_pairs={{0,48},{16,64},{32,80},{48,96},{64,112},{80,0},{96,16},{112,32},{1... | collective-permute-start | bytes 393224 | tf_op jit(solution)/shard_map/ppermute | solution.py:206
  182.1 17.9 %collective-permute-start.13 = (f32[1,256,128]{2,1,0:T(8,128)}, f32[1,256,128]{2,1,0:T(8,128)S(1)}, u32[]{:S(2)}, u32[]{:S(2)}) collective-permute-start(f32[1,256,128]{2,1,0:T(8,128)} %get-tuple-element.48), channel_id=1, source_target_pairs={{0,32},{16,48},{32,64},{48,80},{64,96},{80,112},{96,0},{112,16},{1... | collective-permute-start | bytes 393224 | tf_op jit(solution)/shard_map/ppermute | solution.py:206
  190.7 10.8 %collective-permute-start.14 = (f32[1,256,128]{2,1,0:T(8,128)}, f32[1,256,128]{2,1,0:T(8,128)S(1)}, u32[]{:S(2)}, u32[]{:S(2)}) collective-permute-start(f32[1,256,128]{2,1,0:T(8,128)} %get-tuple-element.49), channel_id=1, source_target_pairs={{0,16},{16,32},{32,48},{48,64},{64,80},{80,96},{96,112},{112,0},{1... | collective-permute-start | bytes 393224 | tf_op jit(solution)/shard_map/ppermute | solution.py:206
  211.5 12.1 %collective-permute-start.15 = (f32[1,256,128]{2,1,0:T(8,128)}, f32[1,256,128]{2,1,0:T(8,128)S(1)}, u32[]{:S(2)}, u32[]{:S(2)}) collective-permute-start(f32[1,256,128]{2,1,0:T(8,128)} %get-tuple-element.51), channel_id=1, source_target_pairs={{0,112},{16,0},{32,16},{48,32},{64,48},{80,64},{96,80},{112,96},{1... | collective-permute-start | bytes 393224 | tf_op jit(solution)/shard_map/ppermute | solution.py:206
  213.1 18.0 %collective-permute-start.16 = (f32[1,256,128]{2,1,0:T(8,128)}, f32[1,256,128]{2,1,0:T(8,128)S(1)}, u32[]{:S(2)}, u32[]{:S(2)}) collective-permute-start(f32[1,256,128]{2,1,0:T(8,128)} %get-tuple-element.52), channel_id=1, source_target_pairs={{0,96},{16,112},{32,0},{48,16},{64,32},{80,48},{96,64},{112,80},{1... | collective-permute-start | bytes 393224 | tf_op jit(solution)/shard_map/ppermute | solution.py:206
  215.5 17.8 %collective-permute-start.17 = (f32[1,256,128]{2,1,0:T(8,128)}, f32[1,256,128]{2,1,0:T(8,128)S(1)}, u32[]{:S(2)}, u32[]{:S(2)}) collective-permute-start(f32[1,256,128]{2,1,0:T(8,128)} %get-tuple-element.53), channel_id=1, source_target_pairs={{0,80},{16,96},{32,112},{48,0},{64,16},{80,32},{96,48},{112,64},{1... | collective-permute-start | bytes 393224 | tf_op jit(solution)/shard_map/ppermute | solution.py:206
  216.5 16.8 %collective-permute-start.18 = (f32[1,256,128]{2,1,0:T(8,128)}, f32[1,256,128]{2,1,0:T(8,128)S(1)}, u32[]{:S(2)}, u32[]{:S(2)}) collective-permute-start(f32[1,256,128]{2,1,0:T(8,128)} %get-tuple-element.54), channel_id=1, source_target_pairs={{0,64},{16,80},{32,96},{48,112},{64,0},{80,16},{96,32},{112,48},{1... | collective-permute-start | bytes 393224 | tf_op jit(solution)/shard_map/ppermute | solution.py:206
  220.4 18.5 %collective-permute-start.19 = (f32[1,256,128]{2,1,0:T(8,128)}, f32[1,256,128]{2,1,0:T(8,128)S(1)}, u32[]{:S(2)}, u32[]{:S(2)}) collective-permute-start(f32[1,256,128]{2,1,0:T(8,128)} %get-tuple-element.55), channel_id=1, source_target_pairs={{0,48},{16,64},{32,80},{48,96},{64,112},{80,0},{96,16},{112,32},{1... | collective-permute-start | bytes 393224 | tf_op jit(solution)/shard_map/ppermute | solution.py:206
  223.7 16.5 %collective-permute-start.20 = (f32[1,256,128]{2,1,0:T(8,128)}, f32[1,256,128]{2,1,0:T(8,128)S(1)}, u32[]{:S(2)}, u32[]{:S(2)}) collective-permute-start(f32[1,256,128]{2,1,0:T(8,128)} %get-tuple-element.56), channel_id=1, source_target_pairs={{0,32},{16,48},{32,64},{48,80},{64,96},{80,112},{96,0},{112,16},{1... | collective-permute-start | bytes 393224 | tf_op jit(solution)/shard_map/ppermute | solution.py:206
  231.1 13.0 %collective-permute-start.21 = (f32[1,256,128]{2,1,0:T(8,128)}, f32[1,256,128]{2,1,0:T(8,128)S(1)}, u32[]{:S(2)}, u32[]{:S(2)}) collective-permute-start(f32[1,256,128]{2,1,0:T(8,128)} %get-tuple-element.57), channel_id=1, source_target_pairs={{0,16},{16,32},{32,48},{48,64},{64,80},{80,96},{96,112},{112,0},{1... | collective-permute-start | bytes 393224 | tf_op jit(solution)/shard_map/ppermute | solution.py:206
  251.5 5.1 %collective-permute-start.23 = (f32[8,128]{1,0:T(8,128)S(1)}, f32[8,128]{1,0:T(8,128)S(1)}, u32[]{:S(2)}, u32[]{:S(2)}) collective-permute-start(f32[8,128]{1,0:T(8,128)S(1)} %get-tuple-element.62), channel_id=1, source_target_pairs={{0,2},{1,3},{2,0},{3,1},{4,6},{5,7},{6,4},{7,5},{8,10},{9,11},{10,... | collective-permute-start | bytes 12296 | tf_op jit(solution)/shard_map/ppermute | solution.py:501
  259.8 5.1 %collective-permute-start.26 = (f32[8,128]{1,0:T(8,128)S(1)}, f32[8,128]{1,0:T(8,128)S(1)}, u32[]{:S(2)}, u32[]{:S(2)}) collective-permute-start(f32[8,128]{1,0:T(8,128)S(1)} %add_add_fusion.3), channel_id=1, source_target_pairs={{0,8},{4,12},{8,0},{12,4},{1,9},{5,13},{9,1},{13,5},{2,10},{6,14},... | collective-permute-start | bytes 12296 | tf_op jit(solution)/shard_map/ppermute | solution.py:501
  264.9 6.1 %collective-permute-start.30 = (f32[8,128]{1,0:T(8,128)S(1)}, f32[8,128]{1,0:T(8,128)S(1)}, u32[]{:S(2)}, u32[]{:S(2)}) collective-permute-start(f32[8,128]{1,0:T(8,128)S(1)} %add_add_fusion.2), channel_id=1, source_target_pairs={{0,16},{16,0},{32,48},{48,32},{64,80},{80,64},{96,112},{112,96},{1... | collective-permute-start | bytes 12296 | tf_op jit(solution)/shard_map/ppermute | solution.py:501
  265.9 5.1 %collective-permute-start.29 = (f32[8,128]{1,0:T(8,128)S(1)}, f32[8,128]{1,0:T(8,128)S(1)}, u32[]{:S(2)}, u32[]{:S(2)}) collective-permute-start(f32[8,128]{1,0:T(8,128)S(1)} %add_add_fusion.2), channel_id=1, source_target_pairs={{0,128},{16,144},{32,160},{48,176},{64,192},{80,208},{96,224},{112... | collective-permute-start | bytes 12296 | tf_op jit(solution)/shard_map/ppermute | solution.py:501
  271.0 7.9 %collective-permute-start.22 = (f32[16,128]{1,0:T(8,128)S(1)}, f32[16,128]{1,0:T(8,128)S(1)}, u32[]{:S(2)}, u32[]{:S(2)}) collective-permute-start(f32[16,128]{1,0:T(8,128)S(1)} %get-tuple-element.61), channel_id=1, source_target_pairs={{0,128},{128,0},{1,129},{129,1},{2,130},{130,2},{3,131},{131,3},{4... | collective-permute-start | bytes 24584 | tf_op jit(solution)/shard_map/ppermute | solution.py:495
  271.0 8.5 %collective-permute-start.33 = (f32[8,128]{1,0:T(8,128)S(1)}, f32[8,128]{1,0:T(8,128)S(1)}, u32[]{:S(2)}, u32[]{:S(2)}) collective-permute-start(f32[8,128]{1,0:T(8,128)S(1)} %add_add_fusion.1), channel_id=1, source_target_pairs={{0,32},{16,48},{32,64},{48,80},{64,96},{80,112},{96,0},{112,16},{1... | collective-permute-start | bytes 12296 | tf_op jit(solution)/shard_map/ppermute | solution.py:501
  272.0 7.5 %collective-permute-start.34 = (f32[8,128]{1,0:T(8,128)S(1)}, f32[8,128]{1,0:T(8,128)S(1)}, u32[]{:S(2)}, u32[]{:S(2)}) collective-permute-start(f32[8,128]{1,0:T(8,128)S(1)} %add_add_fusion.1), channel_id=1, source_target_pairs={{0,96},{16,112},{32,0},{48,16},{64,32},{80,48},{96,64},{112,80},{1... | collective-permute-start | bytes 12296 | tf_op jit(solution)/shard_map/ppermute | solution.py:501
  275.3 7.5 %collective-permute-start.32 = (f32[8,128]{1,0:T(8,128)S(1)}, f32[8,128]{1,0:T(8,128)S(1)}, u32[]{:S(2)}, u32[]{:S(2)}) collective-permute-start(f32[8,128]{1,0:T(8,128)S(1)} %add_add_fusion.1), channel_id=1, source_target_pairs={{0,64},{16,80},{32,96},{48,112},{64,0},{80,16},{96,32},{112,48},{1... | collective-permute-start | bytes 12296 | tf_op jit(solution)/shard_map/ppermute | solution.py:501
  (15 other events, 196.5 us)

commit v2 on v1

--- a/solution.py
+++ b/solution.py
@@ -396,14 +396,22 @@
 
 
 def pack_cols_kernel(vel, out):
-    def body(g, carry):
-        start = pl.multiple_of(g * 16, 16)
+    for g in range(8):
         for c in range(3):
             for p in range(2):
-                out[g, c, p] = vel[c, p, pl.ds(start, 16), :]
-        return carry
-
-    lax.fori_loop(0, 32, body, 0)
+                out[g, c, p] = vel[c, p, 16 * g : 16 * g + 16, :]
+
+
+def pack_cols(velocity):
+    return pl.pallas_call(
+        pack_cols_kernel,
+        out_shape=f32_far(32, 3, 2, 16, 256),
+        grid=(4,),
+        in_specs=[pl.BlockSpec((3, 2, 128, 256), lambda i: (0, 0, i, 0))],
+        out_specs=pl.BlockSpec((8, 3, 2, 16, 256), lambda i: (i, 0, 0, 0, 0)),
+        compiler_params=pltpu.CompilerParams(vmem_limit_bytes=LIMIT),
+        name="pack_cols",
+    )(far(velocity))
 
 
 def partial_kernel(place, y_terms, x_sums, *refs):
@@ -460,7 +468,7 @@
     row = lax.axis_index("row")
     col = lax.axis_index(COL)
     row_arg = row.astype(jnp.int32).reshape(1)
-    for_cols = vmem_call(pack_cols_kernel, f32(32, 3, 2, 16, 256))(velocity)
+    for_cols = pack_cols(velocity)
     lines = lax.all_to_all(for_cols, PLANE_COL, split_axis=0, concat_axis=0, tiled=True)
     v_blocks = pack_rows(row_arg, velocity, (1,))
     v_blocks = send_blocks(v_blocks)

time: 285 us -> 285 us (level)
  Pallas kernels: 48.2 us -> 52.1 us
  local copies, waits for them, and re-layouts: 8.04 us -> 4.52 us
    pallas_call x0 -> x1, Pallas kernels: none -> 4.2 us  [pack_cols(): pl.pallas_call(pack_cols_kernel, out_shape=f32_far(32, 3, 2, 16, 256), gr...]
    unnamed x19 -> x15, local copies, waits for them, and re-layouts: 7.46 us -> 3.94 us
    pallas_call x7 -> x6, Pallas kernels: 40.9 us -> 40.6 us  [call(): pl.pallas_call(kernel, out_shape=list(outs) if many else outs, in_specs=s...]
where the time goes in v2:
time: 285 us; the launch traced here: 284 us
  waiting for transfers between devices  150 us (53%)
  starting transfers between devices  76.4 us (27%)
  Pallas kernels  52.1 us (18%)
  local copies, waits for them, and re-layouts  4.52 us (2%)
    ppermute x21, waiting for transfers between devices, send_blocks(): got[(ROWS - dist) % ROWS] = lax.ppermute(blocks[dist], 'row', perm)  99.6 us
    pallas_call x6, Pallas kernels, call(): pl.pallas_call(kernel, out_shape=list(outs) if many else outs, in_specs=s...  40.6 us
    ppermute x21, starting transfers between devices, send_blocks(): got[(ROWS - dist) % ROWS] = lax.ppermute(blocks[dist], 'row', perm)  38.2 us
    all_to_all x1, waiting for transfers between devices, whole_step(): lax.all_to_all(for_cols, PLANE_COL, split_axis=0, concat_axis=0, tiled=True)  37.9 us
    ppermute x12, starting transfers between devices, sum_of_four(): lax.ppermute(values, axis, [(i, partner(i, n)) for i in range(size)])  19.1 us
    ppermute x12, waiting for transfers between devices, sum_of_four(): lax.ppermute(values, axis, [(i, partner(i, n)) for i in range(size)])  9.58 us
    all_to_all x1, starting transfers between devices, whole_step(): lax.all_to_all(for_cols, PLANE_COL, split_axis=0, concat_axis=0, tiled=True)  7.75 us
    all_to_all x1, starting transfers between devices, whole_step(): lax.all_to_all(y_terms.reshape(32, 2, 2, 16, 256), PLANE_COL, split_axis=...  7 us
  transfers between devices with their start and end apart: 38, of which 21 were waited for; matrix products, arithmetic and copies ran while one was open for 0% of the time, Pallas kernels for 13%

profile of v2, /device:TPU:2, one launch (start us, length us, event | category | flops | bytes accessed | tf_op | source)
XLA Modules:
  0.0 283.8 jit_solution(8940663830091362103)
XLA Ops:
  0.6 4.2 %pack_cols.1 = f32[32,3,2,16,256]{4,3,2,1,0:T(8,128)} custom-call(f32[3,2,512,256]{3,2,1,0:T(8,128)} %refs_0_.3), custom_call_target="tpu_custom_call" | custom-call | tf_op jit(solution)/shard_map/pack_cols/pallas_call | solution.py:406
  4.8 7.8 %all-to-all-start = ((f32[32,3,2,16,256]{4,3,2,1,0:T(8,128)}), f32[32,3,2,16,256]{4,3,2,1,0:T(8,128)S(1)}, u32[]{:S(2)}, u32[]{:S(2)}) async-start(f32[32,3,2,16,256]{4,3,2,1,0:T(8,128)} %pack_cols.1), calls=%async_computation | async-start | bytes 6291456 | tf_op jit(solution)/shard_map/all_to_all | solution.py:472
  13.6 37.9 %all-to-all-done = f32[32,3,2,16,256]{4,3,2,1,0:T(8,128)S(1)} async-done(((f32[32,3,2,16,256]{4,3,2,1,0:T(8,128)}), f32[32,3,2,16,256]{4,3,2,1,0:T(8,128)S(1)}, u32[]{:S(2)}, u32[]{:S(2)}) %all-to-all-start) | async-done | bytes 3145760 | tf_op jit(solution)/shard_map/all_to_all | solution.py:472
  52.5 10.1 %shard_map.59 = f32[2,16,2,2,16,256]{5,4,3,2,1,0:T(8,128)S(1)} custom-call(f32[256,256]{1,0:T(8,128)S(1)} %shard_map.58.base.refs_0_, f32[16,2,1,256]{3,2,1,0:T(1,128)S(1)} %copy-done.6, f32[2,256,128]{2,1,0:T(8,128)S(1)} %copy-done.2, f32[2,16,3,2,16,256]{5,4,3,2,1,0:T(8,128)S(1)} %bitcast.4), custom_call_target="tpu_custom_call" | custom-call | tf_op jit(solution)/shard_map/pallas_call | solution.py:60
  63.9 7.0 %all-to-all-start.1 = ((f32[32,2,2,16,256]{4,3,2,1,0:T(8,128)}), f32[32,2,2,16,256]{4,3,2,1,0:T(8,128)}, u32[]{:S(2)}, u32[]{:S(2)}) async-start(f32[32,2,2,16,256]{4,3,2,1,0:T(8,128)} %bitcast.5), calls=%async_computation.1 | async-start | bytes 4194304 | tf_op jit(solution)/shard_map/all_to_all | solution.py:481
  71.0 3.8 %pack_rows.2 = (f32[2,256,128]{2,1,0:T(8,128)}, f32[2,256,128]{2,1,0:T(8,128)}, f32[2,256,128]{2,1,0:T(8,128)}, f32[2,256,128]{2,1,0:T(8,128)}, f32[2,256,128]{2...) custom-call(s32[1]{0:T(128)} %bitcast.row, f32[3,2,512,256]{3,2,1,0:T(8,128)S(1)} %copy-done, ...), custom_call_target="tpu_custom_call" | custom-call | tf_op jit(solution)/shard_map/pack_rows/pallas_call | solution.py:180
  74.8 5.9 %collective-permute-start = (f32[2,256,128]{2,1,0:T(8,128)}, f32[2,256,128]{2,1,0:T(8,128)S(1)}, u32[]{:S(2)}, u32[]{:S(2)}) collective-permute-start(f32[2,256,128]{2,1,0:T(8,128)} %get-tuple-element.34), channel_id=1, source_target_pairs={{0,112},{16,0},{32,16},{48,32},{64,48},{80,64},{96,80},{112,96},{1... | collective-permute-start | bytes 786440 | tf_op jit(solution)/shard_map/ppermute | solution.py:206
  82.5 5.0 %collective-permute-start.3 = (f32[2,256,128]{2,1,0:T(8,128)}, f32[2,256,128]{2,1,0:T(8,128)S(1)}, u32[]{:S(2)}, u32[]{:S(2)}) collective-permute-start(f32[2,256,128]{2,1,0:T(8,128)} %get-tuple-element.37), channel_id=1, source_target_pairs={{0,64},{16,80},{32,96},{48,112},{64,0},{80,16},{96,32},{112,48},{1... | collective-permute-start | bytes 786440 | tf_op jit(solution)/shard_map/ppermute | solution.py:206
  87.6 6.8 %collective-permute-done.refs_1_.refs_4_ = f32[2,256,128]{2,1,0:T(8,128)S(1)} collective-permute-done((f32[2,256,128]{2,1,0:T(8,128)}, f32[2,256,128]{2,1,0:T(8,128)S(1)}, u32[]{:S(2)}, u32[]{:S(2)}) %collective-permute-start) | collective-permute-done | bytes 262176 | tf_op jit(solution)/shard_map/ppermute | solution.py:206
  94.3 12.7 %collective-permute-done.1.refs_2_.refs_5_ = f32[2,256,128]{2,1,0:T(8,128)S(1)} collective-permute-done((f32[2,256,128]{2,1,0:T(8,128)}, f32[2,256,128]{2,1,0:T(8,128)S(1)}, u32[]{:S(2)}, u32[]{:S(2)}) %collective-permute-start.1) | collective-permute-done | bytes 262176 | tf_op jit(solution)/shard_map/ppermute | solution.py:206
  107.0 19.2 %collective-permute-done.2.refs_3_.refs_6_ = f32[2,256,128]{2,1,0:T(8,128)S(1)} collective-permute-done((f32[2,256,128]{2,1,0:T(8,128)}, f32[2,256,128]{2,1,0:T(8,128)S(1)}, u32[]{:S(2)}, u32[]{:S(2)}) %collective-permute-start.2) | collective-permute-done | bytes 262176 | tf_op jit(solution)/shard_map/ppermute | solution.py:206
  126.2 3.8 %collective-permute-done.5.refs_6_.refs_9_ = f32[2,256,128]{2,1,0:T(8,128)S(1)} collective-permute-done((f32[2,256,128]{2,1,0:T(8,128)}, f32[2,256,128]{2,1,0:T(8,128)S(1)}, u32[]{:S(2)}, u32[]{:S(2)}) %collective-permute-start.5) | collective-permute-done | bytes 262176 | tf_op jit(solution)/shard_map/ppermute | solution.py:206
  130.0 3.7 %collective-permute-done.6.refs_7_.refs_10_ = f32[2,256,128]{2,1,0:T(8,128)S(1)} collective-permute-done((f32[2,256,128]{2,1,0:T(8,128)}, f32[2,256,128]{2,1,0:T(8,128)S(1)}, u32[]{:S(2)}, u32[]{:S(2)}) %collective-permute-start.6) | collective-permute-done | bytes 262176 | tf_op jit(solution)/shard_map/ppermute | solution.py:206
  137.4 10.2 %shard_map.60 = (f32[8,256,128]{2,1,0:T(8,128)S(1)}, f32[8,128]{1,0:T(8,128)S(1)}) custom-call(s32[1]{0:T(128)} %bitcast.row, f32[256,256]{1,0:T(8,128)S(1)} %shard_map.58.base.refs_0_, f32[16,2,1,256]{3,2,1,0:T(1,128)S(1)} %copy-done.6, f32[2,256,128]{2,1,0:T(8,128)S(1)} %copy-done.3, f32[2,256,128]{2,1,0:T(8,128)} %get-tuple-element.33.refs_0_.refs_3_, ...), custom_call_target="tpu_custom_call" | custom-call | tf_op jit(solution)/shard_map/pallas_call | solution.py:60
  148.7 4.2 %all-to-all-start.2 = ((f32[8,256,128]{2,1,0:T(8,128)}), f32[8,256,128]{2,1,0:T(8,128)}, u32[]{:S(2)}, u32[]{:S(2)}) async-start(f32[8,256,128]{2,1,0:T(8,128)} %copy-done.5), calls=%async_computation.2 | async-start | bytes 2097152 | tf_op jit(solution)/shard_map/all_to_all | solution.py:487
  162.5 3.6 %collective-permute-start.11 = (f32[1,256,128]{2,1,0:T(8,128)}, f32[1,256,128]{2,1,0:T(8,128)S(1)}, u32[]{:S(2)}, u32[]{:S(2)}) collective-permute-start(f32[1,256,128]{2,1,0:T(8,128)} %get-tuple-element.46), channel_id=1, source_target_pairs={{0,64},{16,80},{32,96},{48,112},{64,0},{80,16},{96,32},{112,48},{1... | collective-permute-start | bytes 393224 | tf_op jit(solution)/shard_map/ppermute | solution.py:206
  166.3 16.2 %collective-permute-done.8.refs_4_ = f32[1,256,128]{2,1,0:T(8,128)S(1)} collective-permute-done((f32[1,256,128]{2,1,0:T(8,128)}, f32[1,256,128]{2,1,0:T(8,128)S(1)}, u32[]{:S(2)}, u32[]{:S(2)}) %collective-permute-start.8) | collective-permute-done | bytes 131104 | tf_op jit(solution)/shard_map/ppermute | solution.py:206
  184.2 6.9 %collective-permute-done.9.refs_5_ = f32[1,256,128]{2,1,0:T(8,128)S(1)} collective-permute-done((f32[1,256,128]{2,1,0:T(8,128)}, f32[1,256,128]{2,1,0:T(8,128)S(1)}, u32[]{:S(2)}, u32[]{:S(2)}) %collective-permute-start.9) | collective-permute-done | bytes 131104 | tf_op jit(solution)/shard_map/ppermute | solution.py:206
  191.1 5.8 %collective-permute-done.10.refs_6_ = f32[1,256,128]{2,1,0:T(8,128)S(1)} collective-permute-done((f32[1,256,128]{2,1,0:T(8,128)}, f32[1,256,128]{2,1,0:T(8,128)S(1)}, u32[]{:S(2)}, u32[]{:S(2)}) %collective-permute-start.10) | collective-permute-done | bytes 131104 | tf_op jit(solution)/shard_map/ppermute | solution.py:206
  196.9 3.5 %collective-permute-done.13.refs_9_ = f32[1,256,128]{2,1,0:T(8,128)S(1)} collective-permute-done((f32[1,256,128]{2,1,0:T(8,128)}, f32[1,256,128]{2,1,0:T(8,128)S(1)}, u32[]{:S(2)}, u32[]{:S(2)}) %collective-permute-start.13) | collective-permute-done | bytes 131104 | tf_op jit(solution)/shard_map/ppermute | solution.py:206
  201.9 10.0 %shard_map.61 = (f32[1,256,128]{2,1,0:T(8,128)}, f32[1,256,128]{2,1,0:T(8,128)}, f32[1,256,128]{2,1,0:T(8,128)}, f32[1,256,128]{2,1,0:T(8,128)}, f32[1,256,128]{...) custom-call(f32[256,256]{1,0:T(8,128)S(1)} %shard_map.58.base.refs_0_, ...), custom_call_target="tpu_custom_call" | custom-call | tf_op jit(solution)/shard_map/pallas_call | solution.py:60
  216.9 3.8 %collective-permute-start.18 = (f32[1,256,128]{2,1,0:T(8,128)}, f32[1,256,128]{2,1,0:T(8,128)S(1)}, u32[]{:S(2)}, u32[]{:S(2)}) collective-permute-start(f32[1,256,128]{2,1,0:T(8,128)} %get-tuple-element.54), channel_id=1, source_target_pairs={{0,64},{16,80},{32,96},{48,112},{64,0},{80,16},{96,32},{112,48},{1... | collective-permute-start | bytes 393224 | tf_op jit(solution)/shard_map/ppermute | solution.py:206
  220.8 3.3 %collective-permute-start.19 = (f32[1,256,128]{2,1,0:T(8,128)}, f32[1,256,128]{2,1,0:T(8,128)S(1)}, u32[]{:S(2)}, u32[]{:S(2)}) collective-permute-start(f32[1,256,128]{2,1,0:T(8,128)} %get-tuple-element.55), channel_id=1, source_target_pairs={{0,48},{16,64},{32,80},{48,96},{64,112},{80,0},{96,16},{112,32},{1... | collective-permute-start | bytes 393224 | tf_op jit(solution)/shard_map/ppermute | solution.py:206
  224.9 6.6 %collective-permute-done.16.refs_2_ = f32[1,256,128]{2,1,0:T(8,128)S(1)} collective-permute-done((f32[1,256,128]{2,1,0:T(8,128)}, f32[1,256,128]{2,1,0:T(8,128)S(1)}, u32[]{:S(2)}, u32[]{:S(2)}) %collective-permute-start.16) | collective-permute-done | bytes 131104 | tf_op jit(solution)/shard_map/ppermute | solution.py:206
  233.7 5.6 %collective-permute-done.19.refs_5_ = f32[1,256,128]{2,1,0:T(8,128)S(1)} collective-permute-done((f32[1,256,128]{2,1,0:T(8,128)}, f32[1,256,128]{2,1,0:T(8,128)S(1)}, u32[]{:S(2)}, u32[]{:S(2)}) %collective-permute-start.19) | collective-permute-done | bytes 131104 | tf_op jit(solution)/shard_map/ppermute | solution.py:206
  240.6 3.9 %collective-permute-done.21.refs_7_ = f32[1,256,128]{2,1,0:T(8,128)S(1)} collective-permute-done((f32[1,256,128]{2,1,0:T(8,128)}, f32[1,256,128]{2,1,0:T(8,128)S(1)}, u32[]{:S(2)}, u32[]{:S(2)}) %collective-permute-start.21) | collective-permute-done | bytes 131104 | tf_op jit(solution)/shard_map/ppermute | solution.py:206
  244.5 5.3 %shard_map.62 = (f32[2,512,256]{2,1,0:T(8,128)}, f32[8,128]{1,0:T(8,128)S(1)}) custom-call(s32[2]{0:T(128)S(1)} %pad_add_fusion.place, f32[32,2,2,16,256]{4,3,2,1,0:T(8,128)} %all-to-all-done.1.y_terms, f32[8,128]{1,0:T(8,128)S(1)} %get-tuple-element.41.x_sums, f32[1,256,128]{2,1,0:T(8,128)} %get-tuple-element.50.refs_0_, ...), custom_call_target="tpu_custom_call" | custom-call | tf_op jit(solution)/shard_map/pallas_call | solution.py:60
  262.0 3.2 %collective-permute-done.26 = f32[8,128]{1,0:T(8,128)S(1)} collective-permute-done((f32[8,128]{1,0:T(8,128)S(1)}, f32[8,128]{1,0:T(8,128)S(1)}, u32[]{:S(2)}, u32[]{:S(2)}) %collective-permute-start.26) | collective-permute-done | bytes 4128 | tf_op jit(solution)/shard_map/ppermute | solution.py:509
  267.5 3.9 %shard_map.63 = (f32[2,512,256]{2,1,0:T(8,128)}, f32[16,128]{1,0:T(8,128)S(1)}) custom-call(f32[2,512,256]{2,1,0:T(8,128)} %get-tuple-element.58.part, f32[8,256,128]{2,1,0:T(8,128)} %all-to-all-done.2.held), custom_call_target="tpu_custom_call" | custom-call | tf_op jit(solution)/shard_map/pallas_call | solution.py:60
  272.4 3.2 %collective-permute-start.34 = (f32[8,128]{1,0:T(8,128)S(1)}, f32[8,128]{1,0:T(8,128)S(1)}, u32[]{:S(2)}, u32[]{:S(2)}) collective-permute-start(f32[8,128]{1,0:T(8,128)S(1)} %add_add_fusion.1), channel_id=1, source_target_pairs={{0,96},{16,112},{32,0},{48,16},{64,32},{80,48},{96,64},{112,80},{1... | collective-permute-start | bytes 12296 | tf_op jit(solution)/shard_map/ppermute | solution.py:509
  275.6 3.6 %collective-permute-start.32 = (f32[8,128]{1,0:T(8,128)S(1)}, f32[8,128]{1,0:T(8,128)S(1)}, u32[]{:S(2)}, u32[]{:S(2)}) collective-permute-start(f32[8,128]{1,0:T(8,128)S(1)} %add_add_fusion.1), channel_id=1, source_target_pairs={{0,64},{16,80},{32,96},{48,112},{64,0},{80,16},{96,32},{112,48},{1... | collective-permute-start | bytes 12296 | tf_op jit(solution)/shard_map/ppermute | solution.py:509
  279.9 3.2 %collective-permute-done.32 = f32[8,128]{1,0:T(8,128)S(1)} collective-permute-done((f32[8,128]{1,0:T(8,128)S(1)}, f32[8,128]{1,0:T(8,128)S(1)}, u32[]{:S(2)}, u32[]{:S(2)}) %collective-permute-start.32) | collective-permute-done | bytes 4128 | tf_op jit(solution)/shard_map/ppermute | solution.py:509
  (76 shorter events, 48.8 us)
Async XLA Ops:
  4.8 46.7 %all-to-all-start = ((f32[32,3,2,16,256]{4,3,2,1,0:T(8,128)}), f32[32,3,2,16,256]{4,3,2,1,0:T(8,128)S(1)}, u32[]{:S(2)}, u32[]{:S(2)}) async-start(f32[32,3,2,16,256]{4,3,2,1,0:T(8,128)} %pack_cols.1), calls=%async_computation | async-start | bytes 6291456 | tf_op jit(solution)/shard_map/all_to_all | solution.py:472
  63.9 84.7 %all-to-all-start.1 = ((f32[32,2,2,16,256]{4,3,2,1,0:T(8,128)}), f32[32,2,2,16,256]{4,3,2,1,0:T(8,128)}, u32[]{:S(2)}, u32[]{:S(2)}) async-start(f32[32,2,2,16,256]{4,3,2,1,0:T(8,128)} %bitcast.5), calls=%async_computation.1 | async-start | bytes 4194304 | tf_op jit(solution)/shard_map/all_to_all | solution.py:481
  74.8 19.6 %collective-permute-start = (f32[2,256,128]{2,1,0:T(8,128)}, f32[2,256,128]{2,1,0:T(8,128)S(1)}, u32[]{:S(2)}, u32[]{:S(2)}) collective-permute-start(f32[2,256,128]{2,1,0:T(8,128)} %get-tuple-element.34), channel_id=1, source_target_pairs={{0,112},{16,0},{32,16},{48,32},{64,48},{80,64},{96,80},{112,96},{1... | collective-permute-start | bytes 786440 | tf_op jit(solution)/shard_map/ppermute | solution.py:206
  80.6 26.4 %collective-permute-start.1 = (f32[2,256,128]{2,1,0:T(8,128)}, f32[2,256,128]{2,1,0:T(8,128)S(1)}, u32[]{:S(2)}, u32[]{:S(2)}) collective-permute-start(f32[2,256,128]{2,1,0:T(8,128)} %get-tuple-element.35), channel_id=1, source_target_pairs={{0,96},{16,112},{32,0},{48,16},{64,32},{80,48},{96,64},{112,80},{1... | collective-permute-start | bytes 786440 | tf_op jit(solution)/shard_map/ppermute | solution.py:206
  82.1 44.1 %collective-permute-start.2 = (f32[2,256,128]{2,1,0:T(8,128)}, f32[2,256,128]{2,1,0:T(8,128)S(1)}, u32[]{:S(2)}, u32[]{:S(2)}) collective-permute-start(f32[2,256,128]{2,1,0:T(8,128)} %get-tuple-element.36), channel_id=1, source_target_pairs={{0,80},{16,96},{32,112},{48,0},{64,16},{80,32},{96,48},{112,64},{1... | collective-permute-start | bytes 786440 | tf_op jit(solution)/shard_map/ppermute | solution.py:206
  82.5 43.7 %collective-permute-start.3 = (f32[2,256,128]{2,1,0:T(8,128)}, f32[2,256,128]{2,1,0:T(8,128)S(1)}, u32[]{:S(2)}, u32[]{:S(2)}) collective-permute-start(f32[2,256,128]{2,1,0:T(8,128)} %get-tuple-element.37), channel_id=1, source_target_pairs={{0,64},{16,80},{32,96},{48,112},{64,0},{80,16},{96,32},{112,48},{1... | collective-permute-start | bytes 786440 | tf_op jit(solution)/shard_map/ppermute | solution.py:206
  87.6 38.7 %collective-permute-start.4 = (f32[2,256,128]{2,1,0:T(8,128)}, f32[2,256,128]{2,1,0:T(8,128)S(1)}, u32[]{:S(2)}, u32[]{:S(2)}) collective-permute-start(f32[2,256,128]{2,1,0:T(8,128)} %get-tuple-element.38), channel_id=1, source_target_pairs={{0,48},{16,64},{32,80},{48,96},{64,112},{80,0},{96,16},{112,32},{1... | collective-permute-start | bytes 786440 | tf_op jit(solution)/shard_map/ppermute | solution.py:206
  94.3 35.7 %collective-permute-start.5 = (f32[2,256,128]{2,1,0:T(8,128)}, f32[2,256,128]{2,1,0:T(8,128)S(1)}, u32[]{:S(2)}, u32[]{:S(2)}) collective-permute-start(f32[2,256,128]{2,1,0:T(8,128)} %get-tuple-element.39), channel_id=1, source_target_pairs={{0,32},{16,48},{32,64},{48,80},{64,96},{80,112},{96,0},{112,16},{1... | collective-permute-start | bytes 786440 | tf_op jit(solution)/shard_map/ppermute | solution.py:206
  107.0 26.7 %collective-permute-start.6 = (f32[2,256,128]{2,1,0:T(8,128)}, f32[2,256,128]{2,1,0:T(8,128)S(1)}, u32[]{:S(2)}, u32[]{:S(2)}) collective-permute-start(f32[2,256,128]{2,1,0:T(8,128)} %get-tuple-element.40), channel_id=1, source_target_pairs={{0,16},{16,32},{32,48},{48,64},{64,80},{80,96},{96,112},{112,0},{1... | collective-permute-start | bytes 786440 | tf_op jit(solution)/shard_map/ppermute | solution.py:206
  148.7 118.8 %all-to-all-start.2 = ((f32[8,256,128]{2,1,0:T(8,128)}), f32[8,256,128]{2,1,0:T(8,128)}, u32[]{:S(2)}, u32[]{:S(2)}) async-start(f32[8,256,128]{2,1,0:T(8,128)} %copy-done.5), calls=%async_computation.2 | async-start | bytes 2097152 | tf_op jit(solution)/shard_map/all_to_all | solution.py:487
  155.5 27.0 %collective-permute-start.8 = (f32[1,256,128]{2,1,0:T(8,128)}, f32[1,256,128]{2,1,0:T(8,128)S(1)}, u32[]{:S(2)}, u32[]{:S(2)}) collective-permute-start(f32[1,256,128]{2,1,0:T(8,128)} %get-tuple-element.43), channel_id=1, source_target_pairs={{0,112},{16,0},{32,16},{48,32},{64,48},{80,64},{96,80},{112,96},{1... | collective-permute-start | bytes 393224 | tf_op jit(solution)/shard_map/ppermute | solution.py:206
  158.7 32.4 %collective-permute-start.9 = (f32[1,256,128]{2,1,0:T(8,128)}, f32[1,256,128]{2,1,0:T(8,128)S(1)}, u32[]{:S(2)}, u32[]{:S(2)}) collective-permute-start(f32[1,256,128]{2,1,0:T(8,128)} %get-tuple-element.44), channel_id=1, source_target_pairs={{0,96},{16,112},{32,0},{48,16},{64,32},{80,48},{96,64},{112,80},{1... | collective-permute-start | bytes 393224 | tf_op jit(solution)/shard_map/ppermute | solution.py:206
  161.0 35.9 %collective-permute-start.10 = (f32[1,256,128]{2,1,0:T(8,128)}, f32[1,256,128]{2,1,0:T(8,128)S(1)}, u32[]{:S(2)}, u32[]{:S(2)}) collective-permute-start(f32[1,256,128]{2,1,0:T(8,128)} %get-tuple-element.45), channel_id=1, source_target_pairs={{0,80},{16,96},{32,112},{48,0},{64,16},{80,32},{96,48},{112,64},{1... | collective-permute-start | bytes 393224 | tf_op jit(solution)/shard_map/ppermute | solution.py:206
  162.5 34.5 %collective-permute-start.11 = (f32[1,256,128]{2,1,0:T(8,128)}, f32[1,256,128]{2,1,0:T(8,128)S(1)}, u32[]{:S(2)}, u32[]{:S(2)}) collective-permute-start(f32[1,256,128]{2,1,0:T(8,128)} %get-tuple-element.46), channel_id=1, source_target_pairs={{0,64},{16,80},{32,96},{48,112},{64,0},{80,16},{96,32},{112,48},{1... | collective-permute-start | bytes 393224 | tf_op jit(solution)/shard_map/ppermute | solution.py:206
  166.1 30.9 %collective-permute-start.12 = (f32[1,256,128]{2,1,0:T(8,128)}, f32[1,256,128]{2,1,0:T(8,128)S(1)}, u32[]{:S(2)}, u32[]{:S(2)}) collective-permute-start(f32[1,256,128]{2,1,0:T(8,128)} %get-tuple-element.47), channel_id=1, source_target_pairs={{0,48},{16,64},{32,80},{48,96},{64,112},{80,0},{96,16},{112,32},{1... | collective-permute-start | bytes 393224 | tf_op jit(solution)/shard_map/ppermute | solution.py:206
  182.5 17.9 %collective-permute-start.13 = (f32[1,256,128]{2,1,0:T(8,128)}, f32[1,256,128]{2,1,0:T(8,128)S(1)}, u32[]{:S(2)}, u32[]{:S(2)}) collective-permute-start(f32[1,256,128]{2,1,0:T(8,128)} %get-tuple-element.48), channel_id=1, source_target_pairs={{0,32},{16,48},{32,64},{48,80},{64,96},{80,112},{96,0},{112,16},{1... | collective-permute-start | bytes 393224 | tf_op jit(solution)/shard_map/ppermute | solution.py:206
  191.1 10.8 %collective-permute-start.14 = (f32[1,256,128]{2,1,0:T(8,128)}, f32[1,256,128]{2,1,0:T(8,128)S(1)}, u32[]{:S(2)}, u32[]{:S(2)}) collective-permute-start(f32[1,256,128]{2,1,0:T(8,128)} %get-tuple-element.49), channel_id=1, source_target_pairs={{0,16},{16,32},{32,48},{48,64},{64,80},{80,96},{96,112},{112,0},{1... | collective-permute-start | bytes 393224 | tf_op jit(solution)/shard_map/ppermute | solution.py:206
  211.9 12.1 %collective-permute-start.15 = (f32[1,256,128]{2,1,0:T(8,128)}, f32[1,256,128]{2,1,0:T(8,128)S(1)}, u32[]{:S(2)}, u32[]{:S(2)}) collective-permute-start(f32[1,256,128]{2,1,0:T(8,128)} %get-tuple-element.51), channel_id=1, source_target_pairs={{0,112},{16,0},{32,16},{48,32},{64,48},{80,64},{96,80},{112,96},{1... | collective-permute-start | bytes 393224 | tf_op jit(solution)/shard_map/ppermute | solution.py:206
  213.5 18.0 %collective-permute-start.16 = (f32[1,256,128]{2,1,0:T(8,128)}, f32[1,256,128]{2,1,0:T(8,128)S(1)}, u32[]{:S(2)}, u32[]{:S(2)}) collective-permute-start(f32[1,256,128]{2,1,0:T(8,128)} %get-tuple-element.52), channel_id=1, source_target_pairs={{0,96},{16,112},{32,0},{48,16},{64,32},{80,48},{96,64},{112,80},{1... | collective-permute-start | bytes 393224 | tf_op jit(solution)/shard_map/ppermute | solution.py:206
  215.9 17.9 %collective-permute-start.17 = (f32[1,256,128]{2,1,0:T(8,128)}, f32[1,256,128]{2,1,0:T(8,128)S(1)}, u32[]{:S(2)}, u32[]{:S(2)}) collective-permute-start(f32[1,256,128]{2,1,0:T(8,128)} %get-tuple-element.53), channel_id=1, source_target_pairs={{0,80},{16,96},{32,112},{48,0},{64,16},{80,32},{96,48},{112,64},{1... | collective-permute-start | bytes 393224 | tf_op jit(solution)/shard_map/ppermute | solution.py:206
  216.9 16.8 %collective-permute-start.18 = (f32[1,256,128]{2,1,0:T(8,128)}, f32[1,256,128]{2,1,0:T(8,128)S(1)}, u32[]{:S(2)}, u32[]{:S(2)}) collective-permute-start(f32[1,256,128]{2,1,0:T(8,128)} %get-tuple-element.54), channel_id=1, source_target_pairs={{0,64},{16,80},{32,96},{48,112},{64,0},{80,16},{96,32},{112,48},{1... | collective-permute-start | bytes 393224 | tf_op jit(solution)/shard_map/ppermute | solution.py:206
  220.8 18.5 %collective-permute-start.19 = (f32[1,256,128]{2,1,0:T(8,128)}, f32[1,256,128]{2,1,0:T(8,128)S(1)}, u32[]{:S(2)}, u32[]{:S(2)}) collective-permute-start(f32[1,256,128]{2,1,0:T(8,128)} %get-tuple-element.55), channel_id=1, source_target_pairs={{0,48},{16,64},{32,80},{48,96},{64,112},{80,0},{96,16},{112,32},{1... | collective-permute-start | bytes 393224 | tf_op jit(solution)/shard_map/ppermute | solution.py:206
  224.1 16.5 %collective-permute-start.20 = (f32[1,256,128]{2,1,0:T(8,128)}, f32[1,256,128]{2,1,0:T(8,128)S(1)}, u32[]{:S(2)}, u32[]{:S(2)}) collective-permute-start(f32[1,256,128]{2,1,0:T(8,128)} %get-tuple-element.56), channel_id=1, source_target_pairs={{0,32},{16,48},{32,64},{48,80},{64,96},{80,112},{96,0},{112,16},{1... | collective-permute-start | bytes 393224 | tf_op jit(solution)/shard_map/ppermute | solution.py:206
  231.5 13.0 %collective-permute-start.21 = (f32[1,256,128]{2,1,0:T(8,128)}, f32[1,256,128]{2,1,0:T(8,128)S(1)}, u32[]{:S(2)}, u32[]{:S(2)}) collective-permute-start(f32[1,256,128]{2,1,0:T(8,128)} %get-tuple-element.57), channel_id=1, source_target_pairs={{0,16},{16,32},{32,48},{48,64},{64,80},{80,96},{96,112},{112,0},{1... | collective-permute-start | bytes 393224 | tf_op jit(solution)/shard_map/ppermute | solution.py:206
  251.8 5.1 %collective-permute-start.23 = (f32[8,128]{1,0:T(8,128)S(1)}, f32[8,128]{1,0:T(8,128)S(1)}, u32[]{:S(2)}, u32[]{:S(2)}) collective-permute-start(f32[8,128]{1,0:T(8,128)S(1)} %get-tuple-element.62), channel_id=1, source_target_pairs={{0,2},{1,3},{2,0},{3,1},{4,6},{5,7},{6,4},{7,5},{8,10},{9,11},{10,... | collective-permute-start | bytes 12296 | tf_op jit(solution)/shard_map/ppermute | solution.py:509
  260.2 5.1 %collective-permute-start.26 = (f32[8,128]{1,0:T(8,128)S(1)}, f32[8,128]{1,0:T(8,128)S(1)}, u32[]{:S(2)}, u32[]{:S(2)}) collective-permute-start(f32[8,128]{1,0:T(8,128)S(1)} %add_add_fusion.3), channel_id=1, source_target_pairs={{0,8},{4,12},{8,0},{12,4},{1,9},{5,13},{9,1},{13,5},{2,10},{6,14},... | collective-permute-start | bytes 12296 | tf_op jit(solution)/shard_map/ppermute | solution.py:509
  265.3 6.1 %collective-permute-start.30 = (f32[8,128]{1,0:T(8,128)S(1)}, f32[8,128]{1,0:T(8,128)S(1)}, u32[]{:S(2)}, u32[]{:S(2)}) collective-permute-start(f32[8,128]{1,0:T(8,128)S(1)} %add_add_fusion.2), channel_id=1, source_target_pairs={{0,16},{16,0},{32,48},{48,32},{64,80},{80,64},{96,112},{112,96},{1... | collective-permute-start | bytes 12296 | tf_op jit(solution)/shard_map/ppermute | solution.py:509
  266.3 5.1 %collective-permute-start.29 = (f32[8,128]{1,0:T(8,128)S(1)}, f32[8,128]{1,0:T(8,128)S(1)}, u32[]{:S(2)}, u32[]{:S(2)}) collective-permute-start(f32[8,128]{1,0:T(8,128)S(1)} %add_add_fusion.2), channel_id=1, source_target_pairs={{0,128},{16,144},{32,160},{48,176},{64,192},{80,208},{96,224},{112... | collective-permute-start | bytes 12296 | tf_op jit(solution)/shard_map/ppermute | solution.py:509
  271.4 7.9 %collective-permute-start.22 = (f32[16,128]{1,0:T(8,128)S(1)}, f32[16,128]{1,0:T(8,128)S(1)}, u32[]{:S(2)}, u32[]{:S(2)}) collective-permute-start(f32[16,128]{1,0:T(8,128)S(1)} %get-tuple-element.61), channel_id=1, source_target_pairs={{0,128},{128,0},{1,129},{129,1},{2,130},{130,2},{3,131},{131,3},{4... | collective-permute-start | bytes 24584 | tf_op jit(solution)/shard_map/ppermute | solution.py:503
  271.4 8.5 %collective-permute-start.33 = (f32[8,128]{1,0:T(8,128)S(1)}, f32[8,128]{1,0:T(8,128)S(1)}, u32[]{:S(2)}, u32[]{:S(2)}) collective-permute-start(f32[8,128]{1,0:T(8,128)S(1)} %add_add_fusion.1), channel_id=1, source_target_pairs={{0,32},{16,48},{32,64},{48,80},{64,96},{80,112},{96,0},{112,16},{1... | collective-permute-start | bytes 12296 | tf_op jit(solution)/shard_map/ppermute | solution.py:509
  272.4 7.5 %collective-permute-start.34 = (f32[8,128]{1,0:T(8,128)S(1)}, f32[8,128]{1,0:T(8,128)S(1)}, u32[]{:S(2)}, u32[]{:S(2)}) collective-permute-start(f32[8,128]{1,0:T(8,128)S(1)} %add_add_fusion.1), channel_id=1, source_target_pairs={{0,96},{16,112},{32,0},{48,16},{64,32},{80,48},{96,64},{112,80},{1... | collective-permute-start | bytes 12296 | tf_op jit(solution)/shard_map/ppermute | solution.py:509
  275.6 7.5 %collective-permute-start.32 = (f32[8,128]{1,0:T(8,128)S(1)}, f32[8,128]{1,0:T(8,128)S(1)}, u32[]{:S(2)}, u32[]{:S(2)}) collective-permute-start(f32[8,128]{1,0:T(8,128)S(1)} %add_add_fusion.1), channel_id=1, source_target_pairs={{0,64},{16,80},{32,96},{48,112},{64,0},{80,16},{96,32},{112,48},{1... | collective-permute-start | bytes 12296 | tf_op jit(solution)/shard_map/ppermute | solution.py:509
  (13 other events, 192.9 us)
